TPU v7x, 32 devices: a whole 2x2x4 slice. The times are simulated.
32 devices in a mesh: band: 2 (over x), gx: 16 (over z, y, core).
Axes of the slice: x: 2, y: 2, z: 4, core: 2. Of those that a mesh axis runs over, the one named last changes fastest.
Arguments:
- slc_tiles: bfloat16 [64, 2, 64, 2048], P('gx', None, 'band'), parts along dimension 2, may hold values from -64 to 64
- look_weight: float32 [64, 2048], P('band'), parts along dimension 0, may hold values from 0.05 to 1
- pair_list: int32 [192, 2], replicated, may hold values from 0 to 63, as said below
Outputs:
- corrected: float32 [64, 64, 2048], P(None, 'band', 'gx'), parts along dimension 1
There are 2 independent parts, one for each index of `band`. A program takes and returns all parts, laid end to end along the dimension named above; an argument that names none is the same for every part. Nothing has to cross between parts.
Inputs may be any that keep to these rules, and one draw needn't show every extreme that they name: `pair_list`: row p is a pair of date indices; with d = p // 12, the reference date lies in d * 4 to (d + 1) * 4 - 1 and the secondary date is 1 to 4 dates after it.
All inputs are finite; a program needn't handle non-finite values.
Results may differ from a plain program's by a relative error of at most 0.0071.
Values may be sent and summed in bfloat16 or wider, within the bound.
No kernel may reach another device: no remote copies, remote signals or barrier semaphores. Data moves between devices by JAX's collectives and lax.ppermute only.
A program may use at most 128 MiB of HBM per device.

v0:
```python
import jax
import jax.numpy as jnp
from jax import lax
from jax.sharding import PartitionSpec as P

LOOK = 9


def from_behind(block, axis, distance):
    devices = range(lax.axis_size(axis))
    route = [(i - distance, i) for i in devices if i - distance in devices]
    return lax.ppermute(block, axis, route)


def box_sum(values, col_count):
    rim_width = LOOK // 2
    row_count = values.shape[-2]
    padded = jnp.pad(values, [(0, 0)] * (values.ndim - 2) + [(rim_width, rim_width), (0, 0)])
    running = padded[..., 0:row_count, :]
    for offset in range(1, LOOK):
        running = running + padded[..., offset : offset + row_count, :]
    summed = running[..., 0:col_count]
    for offset in range(1, LOOK):
        summed = summed + running[..., offset : offset + col_count]
    return summed


def observe(first_tile, second_tile, weight, col_count):
    first_re = first_tile[..., 0, :, :].astype(jnp.float32)
    first_im = first_tile[..., 1, :, :].astype(jnp.float32)
    second_re = second_tile[..., 0, :, :].astype(jnp.float32)
    second_im = second_tile[..., 1, :, :].astype(jnp.float32)
    cross_re = weight * (first_re * second_re + first_im * second_im)
    cross_im = weight * (first_im * second_re - first_re * second_im)
    power_first = weight * (first_re * first_re + first_im * first_im)
    power_second = weight * (second_re * second_re + second_im * second_im)
    stacked = jnp.stack([cross_re, cross_im, power_first, power_second], axis=0)
    looked = box_sum(stacked, col_count)
    return (looked[1] * lax.rsqrt(looked[2] * looked[3] + 1e-06)).astype(jnp.bfloat16)


def solve_normal(normal_matrix, projected):
    factor = jnp.linalg.cholesky(normal_matrix)
    return jax.scipy.linalg.cho_solve((factor, True), projected)


def body(slc_tiles, look_weight, pair_list):
    rim_width = LOOK // 2
    devices = lax.axis_size("gx")
    position = lax.axis_index("gx")
    date_dev = slc_tiles.shape[0]
    row_count = slc_tiles.shape[2]
    col_total = slc_tiles.shape[3]
    strip_cols = col_total // devices
    pair_total = pair_list.shape[0]
    pair_dev = pair_total // devices
    date_total = date_dev * devices
    weight_pad = jnp.pad(look_weight, ((0, 0), (rim_width, rim_width)))
    following = from_behind(slc_tiles, "gx", -1)
    local_tiles = jnp.concatenate([slc_tiles, following], axis=0)
    local_tiles = jnp.pad(local_tiles, ((0, 0), (0, 0), (0, 0), (rim_width, rim_width)))
    own_pairs = (
        lax.dynamic_slice_in_dim(pair_list, position * pair_dev, pair_dev, 0) - position * date_dev
    )

    def one_pair(pair_row):
        return observe(local_tiles[pair_row[0]], local_tiles[pair_row[1]], weight_pad, col_total)

    observed = lax.map(one_pair, own_pairs)
    blocks = observed.reshape(pair_dev, row_count, devices, strip_cols)
    strips = lax.all_to_all(blocks, "gx", split_axis=2, concat_axis=0, tiled=True)
    strips = strips.reshape(pair_total, row_count * strip_cols)
    date_ids = lax.iota(jnp.int32, date_total)
    incidence = (
        (date_ids[:, None] == pair_list[None, :, 0]).astype(jnp.float32)
        - (date_ids[:, None] == pair_list[None, :, 1]).astype(jnp.float32)
    ).astype(jnp.bfloat16)
    normal_matrix = jnp.dot(incidence, incidence.T, preferred_element_type=jnp.float32) + jnp.eye(
        date_total, dtype=jnp.float32
    )
    projected = jnp.dot(incidence, strips, preferred_element_type=jnp.float32)
    series = solve_normal(normal_matrix, projected).reshape(date_total, row_count, strip_cols)
    column_ids = position * strip_cols + lax.iota(jnp.int32, strip_cols)
    columns = (2.0 * column_ids.astype(jnp.float32) + 1.0) / col_total - 1.0
    all_cols = (2.0 * lax.iota(jnp.int32, col_total).astype(jnp.float32) + 1.0) / col_total - 1.0
    square_sum = jnp.sum(all_cols * all_cols)
    partial_mean = jnp.sum(series, axis=(1, 2))
    partial_slope = jnp.sum(series * columns, axis=(1, 2))
    totals = lax.psum((partial_mean, partial_slope), "gx")
    date_mean = totals[0] / (row_count * col_total)
    date_slope = totals[1] / (row_count * square_sum)
    return series - date_mean[:, None, None] - date_slope[:, None, None] * columns


def solution(mesh):
    return jax.shard_map(
        body,
        mesh=mesh,
        in_specs=(P("gx", None, "band", None), P("band", None), P()),
        out_specs=P(None, "band", "gx"),
        check_vma=False,
    )
```

profile of v0, /device:TPU:0, one launch (start us, length us, event | category | flops | bytes accessed | tf_op | source)
XLA Modules:
  0.0 213.2 jit_solution(9840836476358481530)
XLA Ops:
  0.0 1.3 collective-permute-start
  2.4 1.3 dynamic-slice_subtract_fusion
  4.8 2.6 %fusion.28 = bf16[8,2,32,2056]{3,2,1,0:T(8,128)(2,1)S(1)} fusion(bf16[4,2,32,2048]{3,2,1,0:T(8,128)(2,1)S(1)} %collective-permute-done, bf16[4,2,32,2048]{3,2,1,0:T(8,128)(2,1)} %param.5), kind=kLoop, calls=%fused_computation.57 | loop fusion | flops 9474048 | bytes 4202496 | tf_op jit(solution)/shard_map/concatenate | solution.py:60
  7.3 108.7 %while.12 = (s32[]{:T(128)}, bf16[12,32,2048]{2,1,0:T(8,128)(2,1)}, f32[32,2056]{1,0:T(8,128)S(1)}, s32[12,2]{0,1:T(2,128)}, bf16[8,2,32,2056]{3,2,1,0:T(8,128)(...) while((s32[]{:T(128)}, bf16[12,32,2048]{2,1,0:T(8,128)(2,1)}, f32[32,2056]{1,0:T(8,128)S(1)}, ...), condition=%wide.region_3.4_spmd, body=%wide.region_2.3_spmd.sunk | while | flops 6569993 | bytes 17456360 | solution.py:69
  13.5 2.2 %slice_add_fusion.9 = f32[4,32,2048]{2,1,0:T(8,128)S(1)} fusion(f32[4,32,2056]{2,1,0:T(8,128)S(1)} %fusion.58), kind=kLoop, calls=%fused_computation.17.clone.1 | loop fusion | flops 2097152 | bytes 10485760 | tf_op jit(solution)/shard_map/while/body/eval_jaxpr/add | solution.py:24
  22.5 2.2 %slice_add_fusion.9 = f32[4,32,2048]{2,1,0:T(8,128)S(1)} fusion(f32[4,32,2056]{2,1,0:T(8,128)S(1)} %fusion.58), kind=kLoop, calls=%fused_computation.17.clone.1 | loop fusion | flops 2097152 | bytes 10485760 | tf_op jit(solution)/shard_map/while/body/eval_jaxpr/add | solution.py:24
  31.6 2.2 %slice_add_fusion.9 = f32[4,32,2048]{2,1,0:T(8,128)S(1)} fusion(f32[4,32,2056]{2,1,0:T(8,128)S(1)} %fusion.58), kind=kLoop, calls=%fused_computation.17.clone.1 | loop fusion | flops 2097152 | bytes 10485760 | tf_op jit(solution)/shard_map/while/body/eval_jaxpr/add | solution.py:24
  40.6 2.2 %slice_add_fusion.9 = f32[4,32,2048]{2,1,0:T(8,128)S(1)} fusion(f32[4,32,2056]{2,1,0:T(8,128)S(1)} %fusion.58), kind=kLoop, calls=%fused_computation.17.clone.1 | loop fusion | flops 2097152 | bytes 10485760 | tf_op jit(solution)/shard_map/while/body/eval_jaxpr/add | solution.py:24
  49.7 2.2 %slice_add_fusion.9 = f32[4,32,2048]{2,1,0:T(8,128)S(1)} fusion(f32[4,32,2056]{2,1,0:T(8,128)S(1)} %fusion.58), kind=kLoop, calls=%fused_computation.17.clone.1 | loop fusion | flops 2097152 | bytes 10485760 | tf_op jit(solution)/shard_map/while/body/eval_jaxpr/add | solution.py:24
  58.7 2.2 %slice_add_fusion.9 = f32[4,32,2048]{2,1,0:T(8,128)S(1)} fusion(f32[4,32,2056]{2,1,0:T(8,128)S(1)} %fusion.58), kind=kLoop, calls=%fused_computation.17.clone.1 | loop fusion | flops 2097152 | bytes 10485760 | tf_op jit(solution)/shard_map/while/body/eval_jaxpr/add | solution.py:24
  67.8 2.2 %slice_add_fusion.9 = f32[4,32,2048]{2,1,0:T(8,128)S(1)} fusion(f32[4,32,2056]{2,1,0:T(8,128)S(1)} %fusion.58), kind=kLoop, calls=%fused_computation.17.clone.1 | loop fusion | flops 2097152 | bytes 10485760 | tf_op jit(solution)/shard_map/while/body/eval_jaxpr/add | solution.py:24
  76.8 2.2 %slice_add_fusion.9 = f32[4,32,2048]{2,1,0:T(8,128)S(1)} fusion(f32[4,32,2056]{2,1,0:T(8,128)S(1)} %fusion.58), kind=kLoop, calls=%fused_computation.17.clone.1 | loop fusion | flops 2097152 | bytes 10485760 | tf_op jit(solution)/shard_map/while/body/eval_jaxpr/add | solution.py:24
  85.9 2.2 %slice_add_fusion.9 = f32[4,32,2048]{2,1,0:T(8,128)S(1)} fusion(f32[4,32,2056]{2,1,0:T(8,128)S(1)} %fusion.58), kind=kLoop, calls=%fused_computation.17.clone.1 | loop fusion | flops 2097152 | bytes 10485760 | tf_op jit(solution)/shard_map/while/body/eval_jaxpr/add | solution.py:24
  95.0 2.2 %slice_add_fusion.9 = f32[4,32,2048]{2,1,0:T(8,128)S(1)} fusion(f32[4,32,2056]{2,1,0:T(8,128)S(1)} %fusion.58), kind=kLoop, calls=%fused_computation.17.clone.1 | loop fusion | flops 2097152 | bytes 10485760 | tf_op jit(solution)/shard_map/while/body/eval_jaxpr/add | solution.py:24
  104.0 2.2 %slice_add_fusion.9 = f32[4,32,2048]{2,1,0:T(8,128)S(1)} fusion(f32[4,32,2056]{2,1,0:T(8,128)S(1)} %fusion.58), kind=kLoop, calls=%fused_computation.17.clone.1 | loop fusion | flops 2097152 | bytes 10485760 | tf_op jit(solution)/shard_map/while/body/eval_jaxpr/add | solution.py:24
  113.1 2.2 %slice_add_fusion.9 = f32[4,32,2048]{2,1,0:T(8,128)S(1)} fusion(f32[4,32,2056]{2,1,0:T(8,128)S(1)} %fusion.58), kind=kLoop, calls=%fused_computation.17.clone.1 | loop fusion | flops 2097152 | bytes 10485760 | tf_op jit(solution)/shard_map/while/body/eval_jaxpr/add | solution.py:24
  116.0 3.0 %copy_bitcast_fusion = bf16[12,32,16,128]{3,1,0,2:T(8,128)(2,1)} fusion(bf16[12,32,2048]{2,1,0:T(8,128)(2,1)} %get-tuple-element.70), kind=kLoop, calls=%fused_computation.62 | loop fusion | bytes 3145728 | tf_op jit(solution)/shard_map/reshape | solution.py:70
  119.0 18.4 %all-to-all-start = ((bf16[12,32,16,128]{3,1,0,2:T(8,128)(2,1)}), bf16[12,32,16,128]{3,1,0,2:T(8,128)(2,1)S(1)}, u32[]{:S(2)}, u32[]{:S(2)}) async-start(bf16[12,32,16,128]{3,1,0,2:T(8,128)(2,1)} %copy_bitcast_fusion), calls=%async_computation | async-start | bytes 3145728 | tf_op jit(solution)/shard_map/all_to_all | solution.py:71
  137.7 5.8 %cholesky.17 = f32[64,64]{1,0:T(8,128)S(1)} custom-call(f32[64,64]{1,0:T(8,128)S(1)} %fusion.41), custom_call_target="Cholesky" | custom-call | tf_op jit(solution)/shard_map/jit(cholesky)/cholesky | solution.py:43
  144.9 4.9 %custom-call.10 = f32[1,64,64]{1,2,0:T(8,128)S(1)} custom-call(f32[1,64,64]{2,1,0:T(8,128)S(1)} %fusion.34), custom_call_target="InvertDiagBlocksLowerTriangular" | custom-call | tf_op jit(solution)/shard_map/jit(_cho_solve)/triangular_solve | solution.py:44
  151.1 18.2 %all-to-all-done = bf16[12,32,16,128]{3,1,0,2:T(8,128)(2,1)S(1)} async-done(((bf16[12,32,16,128]{3,1,0,2:T(8,128)(2,1)}), bf16[12,32,16,128]{3,1,0,2:T(8,128)(2,1)S(1)}, u32[]{:S(2)}, u32[]{:S(2)}) %all-to-all-start) | async-done | bytes 1572896 | tf_op jit(solution)/shard_map/all_to_all | solution.py:71
  170.5 2.5 %fusion.38 = f32[32,128,64]{1,2,0:T(8,128)S(1)} fusion(f32[32,128,64]{2,1,0:T(8,128)S(1)} %fusion.29, f32[1,64,64]{1,2,0:T(8,128)S(1)} %custom-call.10), kind=kOutput, calls=%fused_computation.74 | convolution fusion | flops 201326592 | bytes 2113536 | tf_op jit(solution)/shard_map/jit(_cho_solve)/triangular_solve | solution.py:44
  174.2 37.2 %all-reduce.3 = (f32[64]{0:T(128)S(1)}, f32[64]{0:T(128)S(1)}) all-reduce(f32[64]{0:T(128)S(1)} %get-tuple-element.72, f32[64]{0:T(128)S(1)} %get-tuple-element.71), channel_id=1, replica_groups=mesh['band'=2,'gx'=16] {'gx'}, use_global_device_ids=true, to_apply=%region_7.8 | all-reduce | flops 128 | bytes 1024 | tf_op jit(solution)/shard_map/psum | solution.py:89
  211.7 1.6 copy.8
  (91 shorter events, 44.0 us)
Async XLA Ops:
  0.0 4.8 %collective-permute-start = (bf16[4,2,32,2048]{3,2,1,0:T(8,128)(2,1)}, bf16[4,2,32,2048]{3,2,1,0:T(8,128)(2,1)S(1)}, u32[]{:S(2)}, u32[]{:S(2)}) collective-permute-start(bf16[4,2,32,2048]{3,2,1,0:T(8,128)(2,1)} %param.5), channel_id=1, source_target_pairs={{1,0},{2,1},{3,2},{4,3},{5,4},{6,5},{7,6},{8,7},{9,8},{10,9},{11,1... | collective-permute-start | bytes 3145736 | tf_op jit(solution)/shard_map/ppermute | solution.py:12
  119.0 18.4 %copy-start = (s32[192,2]{0,1:T(2,128)S(1)}, s32[192,2]{0,1:T(2,128)}, u32[]{:S(2)}) copy-start(s32[192,2]{0,1:T(2,128)} %param.7) | copy-start | bytes 4612
  119.0 50.3 %all-to-all-start = ((bf16[12,32,16,128]{3,1,0,2:T(8,128)(2,1)}), bf16[12,32,16,128]{3,1,0,2:T(8,128)(2,1)S(1)}, u32[]{:S(2)}, u32[]{:S(2)}) async-start(bf16[12,32,16,128]{3,1,0,2:T(8,128)(2,1)} %copy_bitcast_fusion), calls=%async_computation | async-start | bytes 3145728 | tf_op jit(solution)/shard_map/all_to_all | solution.py:71
where the time goes:
time: 214 us; the launch traced here: 213 us
  other arithmetic  65.1 us (30%)
  loops' own time  45 us (21%)
  blocking collectives  37.2 us (17%)
  local copies, waits for them, and re-layouts  21.2 us (10%)
  starting transfers between devices  19.7 us (9%)
  waiting for transfers between devices  19.2 us (9%)
  matrix products  5.02 us (2%)
    another operation x1, loops' own time, body(): observed = lax.map(one_pair, own_pairs)  45 us
    psum x1, blocking collectives, body(): totals = lax.psum((partial_mean, partial_slope), 'gx')  37.2 us
    add x12, other arithmetic, box_sum(): summed = summed + running[..., offset:offset + col_count]  26.7 us
    all_to_all x1, starting transfers between devices, body(): lax.all_to_all(blocks, 'gx', split_axis=2, concat_axis=0, tiled=True)  18.4 us
    all_to_all x1, waiting for transfers between devices, body(): lax.all_to_all(blocks, 'gx', split_axis=2, concat_axis=0, tiled=True)  18.2 us
    add x12, other arithmetic, box_sum(): running = running + padded[..., offset:offset + row_count, :]  9.79 us
    dynamic_slice x12, local copies, waits for them, and re-layouts, body(): observed = lax.map(one_pair, own_pairs)  9 us
    dynamic_update_slice x12, other arithmetic, body(): observed = lax.map(one_pair, own_pairs)  8.45 us
  transfers between devices with their start and end apart: 2, of which 2 were waited for; matrix products, arithmetic and copies ran while one was open for 7% of the time, Pallas kernels for 0%

commit v1 on v0

v1 whole, which is shorter than its diff:
```python
import functools

import jax
import jax.numpy as jnp
from jax import lax
from jax.experimental import pallas as pl
from jax.experimental.pallas import tpu as pltpu
from jax.sharding import PartitionSpec as P

LOOK = 9
RIM = LOOK // 2
LAGS = 4
SUB = 8
LANES = 128
EDGE = 2 * RIM
HALF = LANES // EDGE

F32 = jnp.float32
BF16 = jnp.bfloat16


def iota2(shape, dim):
    return lax.broadcasted_iota(jnp.int32, shape, dim)


def split2(value):
    high = value.astype(BF16)
    low = (value - high.astype(F32)).astype(BF16)
    return high, low


def window_rows(rows, count):
    def add(a, b):
        return b if a is None else (a if b is None else a + b)

    def at(series, i):
        return series.get(i)

    base = {i: rows[i] for i in range(count)}
    two = {i: add(at(base, i), at(base, i + 1)) for i in range(-RIM, count)}
    four = {i: add(at(two, i), at(two, i + 2)) for i in range(-RIM, count)}
    eight = {i: add(at(four, i), at(four, i + 4)) for i in range(-RIM, count)}
    return [add(at(eight, r - RIM), at(base, r + RIM)) for r in range(count)]


def column_band():
    source = lax.rem(iota2((2 * LANES, LANES), 0), LANES)
    return (jnp.abs(source - iota2((2 * LANES, LANES), 1)) <= RIM).astype(BF16)


def edge_matrix(row_count):
    size = row_count * EDGE
    source, target = iota2((size, size), 0), iota2((size, size), 1)
    near = jnp.abs(source // EDGE - target // EDGE) <= RIM
    e, t = source % EDGE, target % EDGE
    left = (e < RIM) & (t >= RIM) & (e >= t - RIM)
    right = (e >= RIM) & (t < RIM) & (t >= e - RIM)
    return (near & (left | right)).astype(BF16)


def observe_kernel(
    row_count, unit_count,
    pair_ref, next_ref, weight_ref, edge_weight_ref, band_ref, edge_ref, solve_ref, coord_ref,
    series_ref, sums_ref,
    re_s, im_s, pw_s, hre_s, him_s, obs_s,
):
    unit = pl.program_id(0)
    slots = 2 * SUB
    halves = row_count // HALF
    date_dev = next_ref.shape[1] // (2 * row_count)
    hbase = 2 * date_dev * row_count

    def place(block, at):
        for d in range(date_dev):
            for c, dst in ((0, re_s), (1, im_s)):
                start = (d * 2 + c) * row_count
                values = block[start : start + row_count, :].astype(F32)
                for g in range(row_count // SUB):
                    dst[pl.ds(g * SUB * slots + at + d, SUB, stride=slots), :] = values[g * SUB : (g + 1) * SUB]
        edge = block[hbase : hbase + 2 * halves * date_dev, :].astype(F32)
        for c, dst in ((0, hre_s), (1, him_s)):
            for h in range(halves):
                start = (c * halves + h) * date_dev
                dst[pl.ds(h * slots + at, date_dev), :] = edge[start : start + date_dev]

    per_unit = pair_ref.shape[0]
    for s in range(per_unit):
        place(pair_ref[s], s * date_dev)
    place(next_ref[0], per_unit * date_dev)

    def products(re, im, weights, count):
        images = [[] for _ in range(2 + LAGS)]
        for r in range(count):
            w = weights[pl.ds(r, 1), :]
            a_re, a_im = re[pl.ds(r * slots, SUB), :], im[pl.ds(r * slots, SUB), :]
            n_re, n_im = re[pl.ds(r * slots + SUB, SUB), :], im[pl.ds(r * slots + SUB, SUB), :]
            images[0].append(w * (a_re * a_re + a_im * a_im))
            images[1].append(w * (n_re * n_re + n_im * n_im))
        for lag in range(1, LAGS + 1):
            for r in range(count):
                w = weights[pl.ds(r, 1), :]
                a_re, a_im = re[pl.ds(r * slots, SUB), :], im[pl.ds(r * slots, SUB), :]
                b_re, b_im = re[pl.ds(r * slots + lag, SUB), :], im[pl.ds(r * slots + lag, SUB), :]
                images[1 + lag].append(w * (a_im * b_re - a_re * b_im))
        return images

    halo = products(hre_s, him_s, edge_weight_ref, halves)
    halo = jnp.concatenate([jnp.concatenate(image, axis=1) for image in halo], axis=0)
    high, low = split2(halo)
    edge = edge_ref[...]
    edges = jnp.dot(high, edge, preferred_element_type=F32) + jnp.dot(low, edge, preferred_element_type=F32)

    lane = iota2((SUB, LANES), 1)
    at_edge = (lane >= LANES - RIM) | (lane < RIM)
    images = products(re_s, im_s, weight_ref, row_count)
    band = band_ref[...]

    def look(which):
        rows = jnp.concatenate(window_rows(images[which], row_count), axis=0)
        summed = jnp.dot(jnp.concatenate(split2(rows), axis=1), band, preferred_element_type=F32)
        out = []
        for r in range(row_count):
            tile = edges[which * SUB : (which + 1) * SUB, (r // HALF) * LANES : (r // HALF + 1) * LANES]
            shift = (LANES - RIM - EDGE * (r % HALF)) % LANES
            rolled = pltpu.roll(tile, shift, 1)
            out.append(summed[r * SUB : (r + 1) * SUB] + jnp.where(at_edge, rolled, 0.0))
        return out

    for part in range(2):
        for r, value in enumerate(look(part)):
            pw_s[pl.ds(r * slots + part * SUB, SUB), :] = value

    def observed(lag):
        out = []
        for r, value in enumerate(look(1 + lag)):
            p = pw_s[pl.ds(r * slots, SUB), :]
            q = pw_s[pl.ds(r * slots + lag, SUB), :]
            out.append(value * lax.rsqrt(p * q + 1e-06))
        return out

    combos = unit_count * SUB * LAGS
    for lag in range(1, LAGS + 1, 2):
        first, second = observed(lag), observed(lag + 1)
        for r in range(row_count):
            at = pl.multiple_of(r * combos + unit * (SUB * LAGS) + (lag - 1) * SUB, 2 * SUB)
            obs_s[pl.ds(at, 2 * SUB), :] = jnp.concatenate([first[r], second[r]], axis=0).astype(BF16)

    @pl.when(unit == unit_count - 1)
    def _():
        solve = solve_ref[...]
        date_total = solve.shape[0] // 2
        mean = jnp.zeros((date_total, LANES), F32)
        for r in range(row_count):
            both = jnp.dot(solve, obs_s[pl.ds(r * combos, combos), :], preferred_element_type=F32)
            series = both[:date_total] + both[date_total:]
            series_ref[:, r, :] = series
            mean = mean + series
        slope = mean * coord_ref[...]
        sums_ref[:, pl.ds(0, 1)] = jnp.sum(mean, axis=1, keepdims=True)
        sums_ref[:, pl.ds(1, 1)] = jnp.sum(slope, axis=1, keepdims=True)


def observe_all(blocks, weight, edge_weight, solve, coord, row_count, date_dev):
    per_unit = SUB // date_dev
    unit_count = blocks.shape[0] // per_unit
    date_total = unit_count * SUB
    combos = date_total * LAGS
    block_rows = blocks.shape[1]
    halves = row_count // HALF
    slots = 2 * SUB
    whole = lambda a: pl.BlockSpec(a.shape, lambda u: (0,) * a.ndim)
    band, edge = column_band(), edge_matrix(row_count)
    sources = blocks.shape[0]
    return pl.pallas_call(
        functools.partial(observe_kernel, row_count, unit_count),
        grid=(unit_count,),
        out_shape=(
            jax.ShapeDtypeStruct((date_total, row_count, LANES), F32),
            jax.ShapeDtypeStruct((date_total, 2), F32),
        ),
        in_specs=[
            pl.BlockSpec((per_unit, block_rows, LANES), lambda u: (u, 0, 0)),
            pl.BlockSpec((1, block_rows, LANES), lambda u: (lax.rem(u * per_unit + per_unit, sources), 0, 0)),
            whole(weight), whole(edge_weight), whole(band), whole(edge), whole(solve), whole(coord),
        ],
        out_specs=(
            pl.BlockSpec((date_total, row_count, LANES), lambda u: (0, 0, 0)),
            pl.BlockSpec((date_total, 2), lambda u: (0, 0)),
        ),
        scratch_shapes=[
            pltpu.VMEM((row_count * slots, LANES), F32),
            pltpu.VMEM((row_count * slots, LANES), F32),
            pltpu.VMEM((row_count * slots, LANES), F32),
            pltpu.VMEM((halves * slots, LANES), F32),
            pltpu.VMEM((halves * slots, LANES), F32),
            pltpu.VMEM((row_count * combos, LANES), BF16),
        ],
        compiler_params=pltpu.CompilerParams(dimension_semantics=("arbitrary",)),
        name="observe",
    )(blocks, blocks, weight, edge_weight, band, edge, solve, coord)


def solve_matrix(pair_list, date_total):
    first, lag = pair_list[:, 0], pair_list[:, 1] - pair_list[:, 0]
    dates = lax.iota(jnp.int32, date_total)
    at_first = (dates[:, None] == first[None, :]).astype(F32)
    at_second = (dates[:, None] == pair_list[None, :, 1]).astype(F32)
    incidence = (at_first - at_second).astype(BF16)
    normal_matrix = jnp.dot(incidence, incidence.T, preferred_element_type=F32) + jnp.eye(date_total, dtype=F32)
    factor = jnp.linalg.cholesky(normal_matrix)
    lags = lax.iota(jnp.int32, LAGS) + 1
    at_lag = (lags[:, None] == lag[None, :]).astype(BF16)
    count = jnp.dot(at_lag, at_first.astype(BF16).T, preferred_element_type=F32)
    second = dates[None, :] + lags[:, None]
    ends = (dates[:, None, None] == dates[None, None, :]).astype(F32) - (
        dates[:, None, None] == second[None]
    ).astype(F32)
    columns = ends * count[None]
    units = date_total // SUB
    columns = columns.reshape(date_total, LAGS, units, SUB).transpose(0, 2, 1, 3).reshape(date_total, LAGS * date_total)
    solved = jax.scipy.linalg.cho_solve((factor, True), columns)
    return jnp.concatenate(split2(solved), axis=0)


def body(slc_tiles, look_weight, pair_list):
    devices = lax.axis_size("gx")
    position = lax.axis_index("gx")
    date_dev, _, row_count, col_total = slc_tiles.shape
    strip = col_total // devices
    date_total = date_dev * devices
    halves = row_count // HALF

    main = slc_tiles.reshape(date_dev, 2, row_count, devices, strip).transpose(3, 0, 1, 2, 4)
    main = main.reshape(devices, date_dev * 2 * row_count, strip)
    padded = jnp.pad(slc_tiles, ((0, 0), (0, 0), (0, 0), (RIM, RIM)))
    left = padded[..., :col_total].reshape(date_dev, 2, row_count, devices, strip)[..., :RIM]
    right = padded[..., EDGE:].reshape(date_dev, 2, row_count, devices, strip)[..., strip - RIM :]
    halo = jnp.concatenate([left, right], axis=-1).reshape(date_dev, 2, halves, HALF, devices, EDGE)
    halo = halo.transpose(4, 1, 2, 0, 3, 5).reshape(devices, 2 * halves * date_dev, LANES)
    blocks = lax.all_to_all(jnp.concatenate([main, halo], axis=1), "gx", 0, 0, tiled=True)

    weight = lax.dynamic_slice_in_dim(look_weight, position * strip, strip, 1)
    weight_pad = jnp.pad(look_weight, ((0, 0), (RIM, RIM)))
    edge_weight = jnp.concatenate(
        [
            lax.dynamic_slice_in_dim(weight_pad, position * strip, RIM, 1),
            lax.dynamic_slice_in_dim(weight_pad, position * strip + strip + RIM, RIM, 1),
        ],
        axis=1,
    ).reshape(halves, LANES)
    solve = solve_matrix(pair_list, date_total)
    all_cols = (2.0 * lax.iota(jnp.int32, col_total).astype(F32) + 1.0) / col_total - 1.0
    square_sum = jnp.sum(all_cols * all_cols)
    column_ids = position * strip + lax.iota(jnp.int32, strip)
    columns = (2.0 * column_ids.astype(F32) + 1.0) / col_total - 1.0

    series, sums = observe_all(blocks, weight, edge_weight, solve, columns[None], row_count, date_dev)
    step = 1
    while step < devices:
        sums = sums + lax.ppermute(sums, "gx", [(s, s ^ step) for s in range(devices)])
        step *= 2
    date_mean = sums[:, 0] / (row_count * col_total)
    date_slope = sums[:, 1] / (row_count * square_sum)
    return series - date_mean[:, None, None] - date_slope[:, None, None] * columns


def solution(mesh):
    return jax.shard_map(
        body,
        mesh=mesh,
        in_specs=(P("gx", None, "band", None), P("band", None), P()),
        out_specs=P(None, "band", "gx"),
        check_vma=False,
    )
```

time: 214 us -> 76.5 us (0.36)
  loops' own time: 45 us -> 0 us
  other arithmetic: 65.1 us -> 20.5 us
  blocking collectives: 37.2 us -> 0 us
  Pallas kernels: 0 us -> 9.3 us
  waiting for transfers between devices: 19.2 us -> 11.3 us
  local copies, waits for them, and re-layouts: 21.2 us -> 15.8 us
  matrix products: 5.02 us -> 0.81 us
  starting transfers between devices: 19.7 us -> 17.4 us
    another operation x1 -> x0, loops' own time: 45 us -> none  [body(): observed = lax.map(one_pair, own_pairs)]
    psum x1 -> x0, blocking collectives: 37.2 us -> none  [body(): totals = lax.psum((partial_mean, partial_slope), 'gx')]
    add x24 -> x7, other arithmetic: 36.4 us -> 0.87 us  [the longest x4 0.78 us: body(): sums + lax.ppermute(sums, 'gx', [(s, s ^ step) for s in range(devices)])]
    all_to_all x1, waiting for transfers between devices: 18.2 us -> 5.84 us  [body(): lax.all_to_all(jnp.concatenate([main, halo], axis=1), 'gx', 0, 0, tiled=T...]
    all_to_all x1, starting transfers between devices: 18.4 us -> 7.55 us  [body(): lax.all_to_all(jnp.concatenate([main, halo], axis=1), 'gx', 0, 0, tiled=T...]
    pallas_call x0 -> x1, Pallas kernels: none -> 9.3 us  [observe_all(): pl.pallas_call(functools.partial(observe_kernel, row_count, unit_count),...]
    ppermute x1 -> x4, starting transfers between devices: 1.28 us -> 9.81 us  [body(): lax.ppermute(sums, 'gx', [(s, s ^ step) for s in range(devices)])]
    dynamic_update_slice x12 -> x0, other arithmetic: 8.45 us -> none  [body(): observed = lax.map(one_pair, own_pairs)]
  transfers between devices with their start and end apart: 2 -> 5, of which waited for: 2 -> 5; matrix products, arithmetic and copies ran while one was open for 7% -> 24% of each run, Pallas kernels for 0% -> 0%
where the time goes in v1:
time: 76.5 us; the launch traced here: 76 us
  other arithmetic  20.5 us (27%)
  starting transfers between devices  17.4 us (23%)
  local copies, waits for them, and re-layouts  15.8 us (21%)
  waiting for transfers between devices  11.3 us (15%)
  Pallas kernels  9.3 us (12%)
  between operations  0.84 us (1%)
  matrix products  0.81 us (1%)
    ppermute x4, starting transfers between devices, body(): lax.ppermute(sums, 'gx', [(s, s ^ step) for s in range(devices)])  9.81 us
    pallas_call x1, Pallas kernels, observe_all(): pl.pallas_call(functools.partial(observe_kernel, row_count, unit_count),...  9.3 us
    all_to_all x1, starting transfers between devices, body(): lax.all_to_all(jnp.concatenate([main, halo], axis=1), 'gx', 0, 0, tiled=T...  7.55 us
    another operation x3, other arithmetic, solve_matrix(): factor = jnp.linalg.cholesky(normal_matrix)  6.52 us
    all_to_all x1, waiting for transfers between devices, body(): lax.all_to_all(jnp.concatenate([main, halo], axis=1), 'gx', 0, 0, tiled=T...  5.84 us
    another operation x2, other arithmetic, solve_matrix(): solved = jax.scipy.linalg.cho_solve((factor, True), columns)  5.55 us
    ppermute x4, waiting for transfers between devices, body(): lax.ppermute(sums, 'gx', [(s, s ^ step) for s in range(devices)])  5.5 us
    slice x2, local copies, waits for them, and re-layouts, body(): padded[..., :col_total].reshape(date_dev, 2, row_count, devices, strip)  4.25 us
  transfers between devices with their start and end apart: 5, of which 5 were waited for; matrix products, arithmetic and copies ran while one was open for 24% of the time, Pallas kernels for 0%

profile of v1, /device:TPU:0, one launch (start us, length us, event | category | flops | bytes accessed | tf_op | source)
XLA Modules:
  0.0 76.0 jit_solution(13858217676492317299)
XLA Ops:
  0.0 3.3 %pad_slice_fusion.1 = (bf16[4,2,32,2048]{3,2,1,0:T(8,128)(2,1)S(1)}, bf16[4,2,32,2048]{3,2,1,0:T(8,128)(2,1)S(1)}) fusion(bf16[4,2,32,2048]{3,2,1,0:T(8,128)(2,1)} %param.3), kind=kLoop, calls=%fused_computation.4 | loop fusion | bytes 3145728 | tf_op jit(solution)/shard_map/slice | solution.py:236
  3.6 3.1 %copy.24 = bf16[4,2,32,2048]{2,3,1,0:T(8,128)(2,1)} copy(bf16[4,2,32,2048]{3,2,1,0:T(8,128)(2,1)S(1)} %get-tuple-element.16) | data formatting | bytes 2097152 | tf_op jit(solution)/shard_map/reshape | solution.py:237
  6.7 1.0 %slice.53 = bf16[4,2,32,16,4]{2,4,3,1,0:T(4,128)(2,1)S(1)} slice(bf16[4,2,32,16,128]{2,4,3,1,0:T(8,128)(2,1)} %bitcast.37), slice={[0:4], [0:2], [0:32], [0:16], [124:128]} | slice | bytes 65536 | tf_op jit(solution)/shard_map/slice | solution.py:237
  7.7 3.1 %copy.23 = bf16[4,2,32,2048]{2,3,1,0:T(8,128)(2,1)} copy(bf16[4,2,32,2048]{3,2,1,0:T(8,128)(2,1)S(1)} %get-tuple-element.15) | data formatting | bytes 2097152 | tf_op jit(solution)/shard_map/reshape | solution.py:236
  10.8 1.0 %slice.52 = bf16[4,2,32,16,4]{2,4,3,1,0:T(4,128)(2,1)S(1)} slice(bf16[4,2,32,16,128]{2,4,3,1,0:T(8,128)(2,1)} %bitcast.38), slice={[0:4], [0:2], [0:32], [0:16], [0:4]} | slice | bytes 65536 | tf_op jit(solution)/shard_map/slice | solution.py:236
  12.2 0.7 copy.17
  13.2 1.1 %pad_maximum_fusion = bf16[16,272,128]{2,1,0:T(8,128)(2,1)} fusion(bf16[16,16,128]{2,1,0:T(8,128)(2,1)S(1)} %copy.18, bf16[16,256,128]{2,1,0:T(8,128)(2,1)S(1)} %bitcast.39), kind=kLoop, calls=%fused_computation | loop fusion | flops 2228224 | bytes 2228224 | tf_op jit(solution)/shard_map/concatenate | solution.py:240
  14.2 7.5 %all-to-all-start = ((bf16[16,272,128]{2,1,0:T(8,128)(2,1)}), bf16[16,272,128]{2,1,0:T(8,128)(2,1)S(1)}, u32[]{:S(2)}, u32[]{:S(2)}) async-start(bf16[16,272,128]{2,1,0:T(8,128)(2,1)} %pad_maximum_fusion), calls=%async_computation | async-start | bytes 2228224 | tf_op jit(solution)/shard_map/all_to_all | solution.py:240
  22.5 5.8 %cholesky.17 = f32[64,64]{1,0:T(8,128)S(1)} custom-call(f32[64,64]{1,0:T(8,128)S(1)} %fusion.19), custom_call_target="Cholesky" | custom-call | tf_op jit(solution)/shard_map/jit(cholesky)/cholesky | solution.py:210
  31.3 4.9 %custom-call.10 = f32[1,64,64]{1,2,0:T(8,128)S(1)} custom-call(f32[1,64,64]{2,1,0:T(8,128)S(1)} %fusion.9), custom_call_target="InvertDiagBlocksLowerTriangular" | custom-call | tf_op jit(solution)/shard_map/jit(_cho_solve)/triangular_solve | solution.py:221
  38.2 0.7 fusion.7.band_ref
  39.0 0.9 %fusion.3.edge_ref = bf16[256,256]{1,0:T(8,128)(2,1)} fusion(s32[256]{0:T(256)S(1)} %get-tuple-element.22, s32[256]{0:T(256)S(1)} %get-tuple-element.23, s32[256]{0:T(256)S(1)} %get-tuple-element.21, s32[256]{0:T(256)S(1)} %get-tuple-element.24, pred[256]{0:T(512)(128)(4,1)S(1)} %get-tuple-element.19, pred[256]{0:T(512)(128)(4,1)S(1)} %get-tuple-element.20), kind=kLoop, calls=%fused_computation.20 | loop fusion | flops 1441792 | bytes 135680 | tf_op jit(solution)/shard_map/convert_element_type | solution.py:58
  39.9 5.8 %all-to-all-done.pair_ref.next_ref = bf16[16,272,128]{2,1,0:T(8,128)(2,1)S(1)} async-done(((bf16[16,272,128]{2,1,0:T(8,128)(2,1)}), bf16[16,272,128]{2,1,0:T(8,128)(2,1)S(1)}, u32[]{:S(2)}, u32[]{:S(2)}) %all-to-all-start) | async-done | bytes 1114144 | tf_op jit(solution)/shard_map/all_to_all | solution.py:240
  45.7 1.0 %copy-done = bf16[16,272,128]{2,1,0:T(8,128)(2,1)} copy-done((bf16[16,272,128]{2,1,0:T(8,128)(2,1)}, bf16[16,272,128]{2,1,0:T(8,128)(2,1)S(1)}, u32[]{:S(2)}) %copy-start) | copy-done | bytes 1114136
  46.7 9.3 %observe.1 = (f32[64,32,128]{2,1,0:T(8,128)}, f32[64,2]{1,0:T(8,128)}) custom-call(bf16[16,272,128]{2,1,0:T(8,128)(2,1)} %copy-done, bf16[16,272,128]{2,1,0:T(8,128)(2,1)} %copy-done, f32[32,128]{1,0:T(8,128)} %constant_dynamic-slice_fusion.weight_ref, f32[2,128]{1,0:T(2,128)} %reshape.220.edge_weight_ref, bf16[256,128]{1,0:T(8,128)(2,1)} %fusion.7.band_ref, ...), custom_call_target="tpu_custom_call" | custom-call | tf_op jit(solution)/shard_map/observe/pallas_call | solution.py:174
  56.0 0.8 %collective-permute-start = (f32[64,2]{1,0:T(8,128)}, f32[64,2]{1,0:T(8,128)S(1)}, u32[]{:S(2)}, u32[]{:S(2)}) collective-permute-start(f32[64,2]{1,0:T(8,128)} %get-tuple-element.8), channel_id=1, source_target_pairs={{0,1},{1,0},{2,3},{3,2},{4,5},{5,4},{6,7},{7,6},{8,9},{9,8},{10,11... | collective-permute-start | bytes 1544 | tf_op jit(solution)/shard_map/ppermute | solution.py:260
  56.8 1.1 %collective-permute-done = f32[64,2]{1,0:T(8,128)S(1)} collective-permute-done((f32[64,2]{1,0:T(8,128)}, f32[64,2]{1,0:T(8,128)S(1)}, u32[]{:S(2)}, u32[]{:S(2)}) %collective-permute-start) | collective-permute-done | bytes 544 | tf_op jit(solution)/shard_map/ppermute | solution.py:260
  57.9 0.8 %add.167 = f32[64,2]{1,0:T(8,128)S(1)} add(f32[64,2]{1,0:T(8,128)} %get-tuple-element.8, f32[64,2]{1,0:T(8,128)S(1)} %collective-permute-done) | non-fusion elementwise | flops 128 | bytes 1536 | tf_op jit(solution)/shard_map/add | solution.py:260
  58.7 2.1 %collective-permute-start.1 = (f32[64,2]{1,0:T(8,128)S(1)}, f32[64,2]{1,0:T(8,128)S(1)}, u32[]{:S(2)}, u32[]{:S(2)}) collective-permute-start(f32[64,2]{1,0:T(8,128)S(1)} %add.167), channel_id=1, source_target_pairs={{0,2},{1,3},{2,0},{3,1},{4,6},{5,7},{6,4},{7,5},{8,10},{9,11},{10,... | collective-permute-start | bytes 1544 | tf_op jit(solution)/shard_map/ppermute | solution.py:260
  60.7 1.9 %collective-permute-done.1 = f32[64,2]{1,0:T(8,128)S(1)} collective-permute-done((f32[64,2]{1,0:T(8,128)S(1)}, f32[64,2]{1,0:T(8,128)S(1)}, u32[]{:S(2)}, u32[]{:S(2)}) %collective-permute-start.1) | collective-permute-done | bytes 544 | tf_op jit(solution)/shard_map/ppermute | solution.py:260
  62.6 3.5 %collective-permute-start.2 = (f32[64,2]{1,0:T(8,128)S(1)}, f32[64,2]{1,0:T(8,128)S(1)}, u32[]{:S(2)}, u32[]{:S(2)}) collective-permute-start(f32[64,2]{1,0:T(8,128)S(1)} %add.168), channel_id=1, source_target_pairs={{0,4},{1,5},{2,6},{3,7},{4,0},{5,1},{6,2},{7,3},{8,12},{9,13},{10,... | collective-permute-start | bytes 1544 | tf_op jit(solution)/shard_map/ppermute | solution.py:260
  66.1 1.9 %collective-permute-done.2 = f32[64,2]{1,0:T(8,128)S(1)} collective-permute-done((f32[64,2]{1,0:T(8,128)S(1)}, f32[64,2]{1,0:T(8,128)S(1)}, u32[]{:S(2)}, u32[]{:S(2)}) %collective-permute-start.2) | collective-permute-done | bytes 544 | tf_op jit(solution)/shard_map/ppermute | solution.py:260
  68.0 3.5 %collective-permute-start.3 = (f32[64,2]{1,0:T(8,128)S(1)}, f32[64,2]{1,0:T(8,128)S(1)}, u32[]{:S(2)}, u32[]{:S(2)}) collective-permute-start(f32[64,2]{1,0:T(8,128)S(1)} %add.169), channel_id=1, source_target_pairs={{0,8},{1,9},{2,10},{3,11},{4,12},{5,13},{6,14},{7,15},{8,0},{9,1},... | collective-permute-start | bytes 1544 | tf_op jit(solution)/shard_map/ppermute | solution.py:260
  73.6 2.4 %subtract_subtract_fusion = f32[64,32,128]{2,1,0:T(8,128)} fusion(f32[64,32,128]{2,1,0:T(8,128)} %get-tuple-element.7, f32[64,128]{1,0:T(8,128)S(1)} %broadcast_multiply_fusion, f32[64]{0:T(128)S(1)} %get-tuple-element.9), kind=kLoop, calls=%fused_computation.2 | loop fusion | flops 524288 | bytes 2130176 | tf_op jit(solution)/shard_map/sub | solution.py:264
  (49 shorter events, 8.0 us)
Async XLA Ops:
  0.0 3.3 %copy-start.1 = (bf16[4,2,32,2048]{3,2,1,0:T(8,128)(2,1)S(1)}, bf16[4,2,32,2048]{3,2,1,0:T(8,128)(2,1)}, u32[]{:S(2)}) copy-start(bf16[4,2,32,2048]{3,2,1,0:T(8,128)(2,1)} %param.3) | copy-start | bytes 3145732
  14.2 7.6 %copy-start.3 = (s32[192,2]{0,1:T(2,128)S(1)}, s32[192,2]{0,1:T(2,128)}, u32[]{:S(2)}) copy-start(s32[192,2]{0,1:T(2,128)} %param.5) | copy-start | bytes 4612
  14.2 7.8 %copy-start.2 = (f32[32,2048]{1,0:T(8,128)S(1)}, f32[32,2048]{1,0:T(8,128)}, u32[]{:S(2)}) copy-start(f32[32,2048]{1,0:T(8,128)} %param.4) | copy-start | bytes 786436
  14.2 31.5 %all-to-all-start = ((bf16[16,272,128]{2,1,0:T(8,128)(2,1)}), bf16[16,272,128]{2,1,0:T(8,128)(2,1)S(1)}, u32[]{:S(2)}, u32[]{:S(2)}) async-start(bf16[16,272,128]{2,1,0:T(8,128)(2,1)} %pad_maximum_fusion), calls=%async_computation | async-start | bytes 2228224 | tf_op jit(solution)/shard_map/all_to_all | solution.py:240
  45.7 1.0 %copy-start = (bf16[16,272,128]{2,1,0:T(8,128)(2,1)}, bf16[16,272,128]{2,1,0:T(8,128)(2,1)S(1)}, u32[]{:S(2)}) copy-start(bf16[16,272,128]{2,1,0:T(8,128)(2,1)S(1)} %all-to-all-done.pair_ref.next_ref) | copy-start | bytes 3342340
  56.0 1.9 %collective-permute-start = (f32[64,2]{1,0:T(8,128)}, f32[64,2]{1,0:T(8,128)S(1)}, u32[]{:S(2)}, u32[]{:S(2)}) collective-permute-start(f32[64,2]{1,0:T(8,128)} %get-tuple-element.8), channel_id=1, source_target_pairs={{0,1},{1,0},{2,3},{3,2},{4,5},{5,4},{6,7},{7,6},{8,9},{9,8},{10,11... | collective-permute-start | bytes 1544 | tf_op jit(solution)/shard_map/ppermute | solution.py:260
  58.7 4.0 %collective-permute-start.1 = (f32[64,2]{1,0:T(8,128)S(1)}, f32[64,2]{1,0:T(8,128)S(1)}, u32[]{:S(2)}, u32[]{:S(2)}) collective-permute-start(f32[64,2]{1,0:T(8,128)S(1)} %add.167), channel_id=1, source_target_pairs={{0,2},{1,3},{2,0},{3,1},{4,6},{5,7},{6,4},{7,5},{8,10},{9,11},{10,... | collective-permute-start | bytes 1544 | tf_op jit(solution)/shard_map/ppermute | solution.py:260
  62.6 5.4 %collective-permute-start.2 = (f32[64,2]{1,0:T(8,128)S(1)}, f32[64,2]{1,0:T(8,128)S(1)}, u32[]{:S(2)}, u32[]{:S(2)}) collective-permute-start(f32[64,2]{1,0:T(8,128)S(1)} %add.168), channel_id=1, source_target_pairs={{0,4},{1,5},{2,6},{3,7},{4,0},{5,1},{6,2},{7,3},{8,12},{9,13},{10,... | collective-permute-start | bytes 1544 | tf_op jit(solution)/shard_map/ppermute | solution.py:260
  68.0 5.3 %collective-permute-start.3 = (f32[64,2]{1,0:T(8,128)S(1)}, f32[64,2]{1,0:T(8,128)S(1)}, u32[]{:S(2)}, u32[]{:S(2)}) collective-permute-start(f32[64,2]{1,0:T(8,128)S(1)} %add.169), channel_id=1, source_target_pairs={{0,8},{1,9},{2,10},{3,11},{4,12},{5,13},{6,14},{7,15},{8,0},{9,1},... | collective-permute-start | bytes 1544 | tf_op jit(solution)/shard_map/ppermute | solution.py:260

commit v2 on v1

--- a/solution.py
+++ b/solution.py
@@ -155,9 +155,10 @@
             series = both[:date_total] + both[date_total:]
             series_ref[:, r, :] = series
             mean = mean + series
-        slope = mean * coord_ref[...]
-        sums_ref[:, pl.ds(0, 1)] = jnp.sum(mean, axis=1, keepdims=True)
-        sums_ref[:, pl.ds(1, 1)] = jnp.sum(slope, axis=1, keepdims=True)
+        eye = iota2((date_total, date_total), 0) == iota2((date_total, date_total), 1)
+        for i, part in enumerate((mean, mean * coord_ref[...])):
+            column = jnp.sum(part, axis=1, keepdims=True)
+            sums_ref[pl.ds(i, 1), :] = jnp.sum(jnp.where(eye, column, 0.0), axis=0, keepdims=True)
 
 
 def observe_all(blocks, weight, edge_weight, solve, coord, row_count, date_dev):
@@ -176,7 +177,7 @@
         grid=(unit_count,),
         out_shape=(
             jax.ShapeDtypeStruct((date_total, row_count, LANES), F32),
-            jax.ShapeDtypeStruct((date_total, 2), F32),
+            jax.ShapeDtypeStruct((2, date_total), F32),
         ),
         in_specs=[
             pl.BlockSpec((per_unit, block_rows, LANES), lambda u: (u, 0, 0)),
@@ -185,7 +186,7 @@
         ],
         out_specs=(
             pl.BlockSpec((date_total, row_count, LANES), lambda u: (0, 0, 0)),
-            pl.BlockSpec((date_total, 2), lambda u: (0, 0)),
+            pl.BlockSpec((2, date_total), lambda u: (0, 0)),
         ),
         scratch_shapes=[
             pltpu.VMEM((row_count * slots, LANES), F32),
@@ -198,6 +199,59 @@
         compiler_params=pltpu.CompilerParams(dimension_semantics=("arbitrary",)),
         name="observe",
     )(blocks, blocks, weight, edge_weight, band, edge, solve, coord)
+
+
+def pack_kernel(date_dev, row_count, tiles_ref, out_ref):
+    strips = out_ref.shape[0]
+    size = tiles_ref.shape[0]
+    halves = row_count // HALF
+    source, lane = iota2((2 * LANES, LANES), 0), iota2((2 * LANES, LANES), 1) % EDGE
+    spread = (lane == jnp.where(source < LANES, source - (LANES - RIM), source - LANES + RIM)) & (
+        (source >= LANES) == (lane >= RIM)
+    )
+    spread = spread.astype(BF16)
+    mask = iota2((size, LANES), 0) % HALF == iota2((size, LANES), 1) // EDGE
+    out_rows = 2 * halves * date_dev
+    target, row = iota2((out_rows, size), 0), iota2((out_rows, size), 1)
+    same = (
+        (target % date_dev == row // (2 * row_count))
+        & (target // (halves * date_dev) == row // row_count % 2)
+        & (target // date_dev % halves == row // HALF % halves)
+    ).astype(BF16)
+    nothing = jnp.zeros((size, LANES), BF16)
+    for j in range(strips):
+        out_ref[j, pl.ds(0, size), :] = tiles_ref[:, j * LANES : (j + 1) * LANES]
+        before = tiles_ref[:, (j - 1) * LANES : j * LANES] if j else nothing
+        after = tiles_ref[:, (j + 1) * LANES : (j + 2) * LANES] if j + 1 < strips else nothing
+        copies = jnp.dot(jnp.concatenate([before, after], axis=1), spread, preferred_element_type=F32)
+        copies = jnp.where(mask, copies, 0.0).astype(BF16)
+        edge = jnp.dot(same, copies, preferred_element_type=F32)
+        out_ref[j, pl.ds(size, out_rows), :] = edge.astype(BF16)
+
+
+def pack(tiles, devices):
+    date_dev, _, row_count, col_total = tiles.shape
+    size = date_dev * 2 * row_count
+    block_rows = size + 2 * (row_count // HALF) * date_dev
+    return pl.pallas_call(
+        functools.partial(pack_kernel, date_dev, row_count),
+        out_shape=jax.ShapeDtypeStruct((devices, block_rows, LANES), BF16),
+        in_specs=[pl.BlockSpec(memory_space=pltpu.VMEM)],
+        out_specs=pl.BlockSpec(memory_space=pltpu.VMEM),
+        name="pack",
+    )(tiles.reshape(size, col_total))
+
+
+def remove_kernel(pixels, series_ref, sums_ref, coord_ref, out_ref):
+    dates = series_ref.shape[0]
+    eye = iota2((dates, dates), 0) == iota2((dates, dates), 1)
+    mean = jnp.sum(jnp.where(eye, sums_ref[pl.ds(0, 1), :], 0.0), axis=1, keepdims=True) / pixels
+    slope = jnp.sum(jnp.where(eye, sums_ref[pl.ds(1, 1), :], 0.0), axis=1, keepdims=True)
+    coord = coord_ref[pl.ds(0, 1), :]
+    slope = slope / coord_ref[pl.ds(1, 1), pl.ds(0, 1)]
+    trend = mean + slope * coord
+    for r in range(series_ref.shape[1]):
+        out_ref[:, r, :] = series_ref[:, r, :] - trend
 
 
 def solve_matrix(pair_list, date_total):
@@ -230,14 +284,7 @@
     date_total = date_dev * devices
     halves = row_count // HALF
 
-    main = slc_tiles.reshape(date_dev, 2, row_count, devices, strip).transpose(3, 0, 1, 2, 4)
-    main = main.reshape(devices, date_dev * 2 * row_count, strip)
-    padded = jnp.pad(slc_tiles, ((0, 0), (0, 0), (0, 0), (RIM, RIM)))
-    left = padded[..., :col_total].reshape(date_dev, 2, row_count, devices, strip)[..., :RIM]
-    right = padded[..., EDGE:].reshape(date_dev, 2, row_count, devices, strip)[..., strip - RIM :]
-    halo = jnp.concatenate([left, right], axis=-1).reshape(date_dev, 2, halves, HALF, devices, EDGE)
-    halo = halo.transpose(4, 1, 2, 0, 3, 5).reshape(devices, 2 * halves * date_dev, LANES)
-    blocks = lax.all_to_all(jnp.concatenate([main, halo], axis=1), "gx", 0, 0, tiled=True)
+    blocks = lax.all_to_all(pack(slc_tiles, devices), "gx", 0, 0, tiled=True)
 
     weight = lax.dynamic_slice_in_dim(look_weight, position * strip, strip, 1)
     weight_pad = jnp.pad(look_weight, ((0, 0), (RIM, RIM)))
@@ -259,9 +306,20 @@
     while step < devices:
         sums = sums + lax.ppermute(sums, "gx", [(s, s ^ step) for s in range(devices)])
         step *= 2
-    date_mean = sums[:, 0] / (row_count * col_total)
-    date_slope = sums[:, 1] / (row_count * square_sum)
-    return series - date_mean[:, None, None] - date_slope[:, None, None] * columns
+    trend_coord = jnp.stack([columns, jnp.broadcast_to(row_count * square_sum, (strip,))])
+    rows = SUB
+    return pl.pallas_call(
+        functools.partial(remove_kernel, row_count * col_total),
+        grid=(row_count // rows,),
+        out_shape=jax.ShapeDtypeStruct(series.shape, F32),
+        in_specs=[
+            pl.BlockSpec((date_total, rows, strip), lambda i: (0, i, 0)),
+            pl.BlockSpec(sums.shape, lambda i: (0, 0)),
+            pl.BlockSpec(trend_coord.shape, lambda i: (0, 0)),
+        ],
+        out_specs=pl.BlockSpec((date_total, rows, strip), lambda i: (0, i, 0)),
+        name="remove",
+    )(series, sums, trend_coord)
 
 
 def solution(mesh):

time: 76.5 us -> 68.1 us (0.89)
  local copies, waits for them, and re-layouts: 15.8 us -> 3.44 us
  Pallas kernels: 9.3 us -> 18.1 us
  other arithmetic: 20.5 us -> 17.2 us
  waiting for transfers between devices: 11.3 us -> 9.97 us
    pallas_call x0 -> x2, Pallas kernels: none -> 8.75 us  [the longest x1 4.64 us: pack(): pl.pallas_call(functools.partial(pack_kernel, date_dev, row_count), out_s...]
    reshape x5 -> x0, local copies, waits for them, and re-layouts: 6.96 us -> none  [the longest x1 3.11 us: body(): padded[..., EDGE:].reshape(date_dev, 2, row_count, devices, strip)]
    slice x3 -> x0, local copies, waits for them, and re-layouts: 5.27 us -> none  [the longest x2 4.25 us: body(): padded[..., :col_total].reshape(date_dev, 2, row_count, devices, strip)]
    sub x1 -> x0, other arithmetic: 2.36 us -> none  [body(): series - date_mean[:, None, None] - date_slope[:, None, None] * columns]
    ppermute x4, waiting for transfers between devices: 5.5 us -> 4.13 us  [body(): lax.ppermute(sums, 'gx', [(s, s ^ step) for s in range(devices)])]
    concatenate x2 -> x0, other arithmetic: 1.24 us -> none  [the longest x1 1.07 us: body(): jnp.concatenate([main, halo], axis=1)]
  transfers between devices with their start and end apart: 5 -> 5, of which waited for: 5 -> 4; matrix products, arithmetic and copies ran while one was open for 24% -> 28% of each run, Pallas kernels for 0% -> 0%
where the time goes in v2:
time: 68.1 us; the launch traced here: 67.6 us
  Pallas kernels  18.1 us (27%)
  starting transfers between devices  17.4 us (26%)
  other arithmetic  17.2 us (25%)
  waiting for transfers between devices  9.97 us (15%)
  local copies, waits for them, and re-layouts  3.44 us (5%)
  matrix products  0.81 us (1%)
  between operations  0.81 us (1%)
    ppermute x4, starting transfers between devices, body(): lax.ppermute(sums, 'gx', [(s, s ^ step) for s in range(devices)])  9.81 us
    pallas_call x1, Pallas kernels, observe_all(): pl.pallas_call(functools.partial(observe_kernel, row_count, unit_count),...  9.35 us
    all_to_all x1, starting transfers between devices, body(): blocks = lax.all_to_all(pack(slc_tiles, devices), 'gx', 0, 0, tiled=True)  7.55 us
    another operation x3, other arithmetic, solve_matrix(): factor = jnp.linalg.cholesky(normal_matrix)  6.52 us
    all_to_all x1, waiting for transfers between devices, body(): blocks = lax.all_to_all(pack(slc_tiles, devices), 'gx', 0, 0, tiled=True)  5.84 us
    another operation x2, other arithmetic, solve_matrix(): solved = jax.scipy.linalg.cho_solve((factor, True), columns)  5.55 us
    pallas_call x1, Pallas kernels, pack(): pl.pallas_call(functools.partial(pack_kernel, date_dev, row_count), out_s...  4.64 us
    ppermute x4, waiting for transfers between devices, body(): lax.ppermute(sums, 'gx', [(s, s ^ step) for s in range(devices)])  4.13 us
  transfers between devices with their start and end apart: 5, of which 4 were waited for; matrix products, arithmetic and copies ran while one was open for 28% of the time, Pallas kernels for 0%

profile of v2, /device:TPU:0, one launch (start us, length us, event | category | flops | bytes accessed | tf_op | source)
XLA Modules:
  0.0 67.6 jit_solution(4720288056443943467)
XLA Ops:
  0.0 4.6 %pack.1 = bf16[16,272,128]{2,1,0:T(8,128)(2,1)} custom-call(bf16[256,2048]{1,0:T(8,128)(2,1)} %bitcast.22), custom_call_target="tpu_custom_call" | custom-call | tf_op jit(solution)/shard_map/pack/pallas_call | solution.py:236
  4.6 7.5 %all-to-all-start = ((bf16[16,272,128]{2,1,0:T(8,128)(2,1)}), bf16[16,272,128]{2,1,0:T(8,128)(2,1)S(1)}, u32[]{:S(2)}, u32[]{:S(2)}) async-start(bf16[16,272,128]{2,1,0:T(8,128)(2,1)} %pack.1), calls=%async_computation | async-start | bytes 2228224 | tf_op jit(solution)/shard_map/all_to_all | solution.py:287
  12.9 5.8 %cholesky.17 = f32[64,64]{1,0:T(8,128)S(1)} custom-call(f32[64,64]{1,0:T(8,128)S(1)} %fusion.18), custom_call_target="Cholesky" | custom-call | tf_op jit(solution)/shard_map/jit(cholesky)/cholesky | solution.py:264
  18.8 0.6 compare_reduce_fusion
  19.4 0.7 fusion.9
  20.9 0.7 reshape.147.edge_weight_ref
  21.7 4.9 %custom-call.10 = f32[1,64,64]{1,2,0:T(8,128)S(1)} custom-call(f32[1,64,64]{2,1,0:T(8,128)S(1)} %fusion.9), custom_call_target="InvertDiagBlocksLowerTriangular" | custom-call | tf_op jit(solution)/shard_map/jit(_cho_solve)/triangular_solve | solution.py:275
  26.6 0.6 constant_dynamic-slice_fusion.weight_ref
  28.0 0.6 pad_maximum_fusion.solve_ref
  28.6 0.7 %fusion.7.band_ref = bf16[256,128]{1,0:T(8,128)(2,1)} fusion(s32[256]{0:T(256)S(1)} %iota_and_fusion.1), kind=kLoop, calls=%fused_computation.21 | loop fusion | flops 131072 | bytes 66560 | tf_op jit(solution)/shard_map/convert_element_type | solution.py:48
  29.4 0.9 %fusion.3.edge_ref = bf16[256,256]{1,0:T(8,128)(2,1)} fusion(s32[256]{0:T(256)S(1)} %get-tuple-element.18, s32[256]{0:T(256)S(1)} %get-tuple-element.19, s32[256]{0:T(256)S(1)} %get-tuple-element.17, s32[256]{0:T(256)S(1)} %get-tuple-element.20, pred[256]{0:T(512)(128)(4,1)S(1)} %get-tuple-element.15, pred[256]{0:T(512)(128)(4,1)S(1)} %get-tuple-element.16), kind=kLoop, calls=%fused_computation.14 | loop fusion | flops 1441792 | bytes 135680 | tf_op jit(solution)/shard_map/convert_element_type | solution.py:58
  30.3 5.8 %all-to-all-done.pair_ref.next_ref = bf16[16,272,128]{2,1,0:T(8,128)(2,1)S(1)} async-done(((bf16[16,272,128]{2,1,0:T(8,128)(2,1)}), bf16[16,272,128]{2,1,0:T(8,128)(2,1)S(1)}, u32[]{:S(2)}, u32[]{:S(2)}) %all-to-all-start) | async-done | bytes 1114144 | tf_op jit(solution)/shard_map/all_to_all | solution.py:287
  36.1 1.0 %copy-done = bf16[16,272,128]{2,1,0:T(8,128)(2,1)} copy-done((bf16[16,272,128]{2,1,0:T(8,128)(2,1)}, bf16[16,272,128]{2,1,0:T(8,128)(2,1)S(1)}, u32[]{:S(2)}) %copy-start) | copy-done | bytes 1114136
  37.1 9.4 %observe.1 = (f32[64,32,128]{2,1,0:T(8,128)}, f32[2,64]{1,0:T(2,128)}) custom-call(bf16[16,272,128]{2,1,0:T(8,128)(2,1)} %copy-done, bf16[16,272,128]{2,1,0:T(8,128)(2,1)} %copy-done, f32[32,128]{1,0:T(8,128)} %constant_dynamic-slice_fusion.weight_ref, f32[2,128]{1,0:T(2,128)} %reshape.147.edge_weight_ref, bf16[256,128]{1,0:T(8,128)(2,1)} %fusion.7.band_ref, ...), custom_call_target="tpu_custom_call" | custom-call | tf_op jit(solution)/shard_map/observe/pallas_call | solution.py:175
  46.5 0.8 %collective-permute-start = (f32[2,64]{1,0:T(2,128)}, f32[2,64]{1,0:T(2,128)S(1)}, u32[]{:S(2)}, u32[]{:S(2)}) collective-permute-start(f32[2,64]{1,0:T(2,128)} %get-tuple-element.8), channel_id=1, source_target_pairs={{0,1},{1,0},{2,3},{3,2},{4,5},{5,4},{6,7},{7,6},{8,9},{9,8},{10,11... | collective-permute-start | bytes 1544 | tf_op jit(solution)/shard_map/ppermute | solution.py:307
  47.3 1.0 %collective-permute-done = f32[2,64]{1,0:T(2,128)S(1)} collective-permute-done((f32[2,64]{1,0:T(2,128)}, f32[2,64]{1,0:T(2,128)S(1)}, u32[]{:S(2)}, u32[]{:S(2)}) %collective-permute-start) | collective-permute-done | bytes 544 | tf_op jit(solution)/shard_map/ppermute | solution.py:307
  48.3 0.7 add.149
  49.0 2.1 %collective-permute-start.1 = (f32[2,64]{1,0:T(2,128)S(1)}, f32[2,64]{1,0:T(2,128)S(1)}, u32[]{:S(2)}, u32[]{:S(2)}) collective-permute-start(f32[2,64]{1,0:T(2,128)S(1)} %add.149), channel_id=1, source_target_pairs={{0,2},{1,3},{2,0},{3,1},{4,6},{5,7},{6,4},{7,5},{8,10},{9,11},{10,... | collective-permute-start | bytes 1544 | tf_op jit(solution)/shard_map/ppermute | solution.py:307
  51.0 1.6 %collective-permute-done.1 = f32[2,64]{1,0:T(2,128)S(1)} collective-permute-done((f32[2,64]{1,0:T(2,128)S(1)}, f32[2,64]{1,0:T(2,128)S(1)}, u32[]{:S(2)}, u32[]{:S(2)}) %collective-permute-start.1) | collective-permute-done | bytes 544 | tf_op jit(solution)/shard_map/ppermute | solution.py:307
  52.6 3.5 %collective-permute-start.2 = (f32[2,64]{1,0:T(2,128)S(1)}, f32[2,64]{1,0:T(2,128)S(1)}, u32[]{:S(2)}, u32[]{:S(2)}) collective-permute-start(f32[2,64]{1,0:T(2,128)S(1)} %add.150), channel_id=1, source_target_pairs={{0,4},{1,5},{2,6},{3,7},{4,0},{5,1},{6,2},{7,3},{8,12},{9,13},{10,... | collective-permute-start | bytes 1544 | tf_op jit(solution)/shard_map/ppermute | solution.py:307
  56.1 1.6 %collective-permute-done.2 = f32[2,64]{1,0:T(2,128)S(1)} collective-permute-done((f32[2,64]{1,0:T(2,128)S(1)}, f32[2,64]{1,0:T(2,128)S(1)}, u32[]{:S(2)}, u32[]{:S(2)}) %collective-permute-start.2) | collective-permute-done | bytes 544 | tf_op jit(solution)/shard_map/ppermute | solution.py:307
  57.7 3.5 %collective-permute-start.3 = (f32[2,64]{1,0:T(2,128)S(1)}, f32[2,64]{1,0:T(2,128)S(1)}, u32[]{:S(2)}, u32[]{:S(2)}) collective-permute-start(f32[2,64]{1,0:T(2,128)S(1)} %add.151), channel_id=1, source_target_pairs={{0,8},{1,9},{2,10},{3,11},{4,12},{5,13},{6,14},{7,15},{8,0},{9,1},... | collective-permute-start | bytes 1544 | tf_op jit(solution)/shard_map/ppermute | solution.py:307
  61.1 0.6 multiply_reduce_fusion
  63.5 4.1 %remove.1 = f32[64,32,128]{2,1,0:T(8,128)} custom-call(f32[64,32,128]{2,1,0:T(8,128)} %get-tuple-element.7.series_ref, f32[2,64]{1,0:T(2,128)} %add.152.sums_ref, f32[2,128]{1,0:T(2,128)} %stack.4.coord_ref), custom_call_target="tpu_custom_call" | custom-call | tf_op jit(solution)/shard_map/remove/pallas_call | solution.py:311
  (37 shorter events, 3.5 us)
Async XLA Ops:
  4.6 7.6 %copy-start.3 = (s32[192,2]{0,1:T(2,128)S(1)}, s32[192,2]{0,1:T(2,128)}, u32[]{:S(2)}) copy-start(s32[192,2]{0,1:T(2,128)} %param.5) | copy-start | bytes 4612
  4.6 7.8 %copy-start.1 = (f32[32,2048]{1,0:T(8,128)S(1)}, f32[32,2048]{1,0:T(8,128)}, u32[]{:S(2)}) copy-start(f32[32,2048]{1,0:T(8,128)} %param.4) | copy-start | bytes 786436
  4.6 31.5 %all-to-all-start = ((bf16[16,272,128]{2,1,0:T(8,128)(2,1)}), bf16[16,272,128]{2,1,0:T(8,128)(2,1)S(1)}, u32[]{:S(2)}, u32[]{:S(2)}) async-start(bf16[16,272,128]{2,1,0:T(8,128)(2,1)} %pack.1), calls=%async_computation | async-start | bytes 2228224 | tf_op jit(solution)/shard_map/all_to_all | solution.py:287
  30.3 32.1 %copy-start.2 = (f32[1,128]{1,0:T(1,128)S(1)}, f32[1,128]{1,0:T(1,128)}, u32[]{:S(2)}) copy-start(f32[1,128]{1,0:T(1,128)} %multiply_add_fusion.1.coord_ref) | copy-start | bytes 1540
  36.1 1.0 %copy-start = (bf16[16,272,128]{2,1,0:T(8,128)(2,1)}, bf16[16,272,128]{2,1,0:T(8,128)(2,1)S(1)}, u32[]{:S(2)}) copy-start(bf16[16,272,128]{2,1,0:T(8,128)(2,1)S(1)} %all-to-all-done.pair_ref.next_ref) | copy-start | bytes 3342340
  46.5 1.8 %collective-permute-start = (f32[2,64]{1,0:T(2,128)}, f32[2,64]{1,0:T(2,128)S(1)}, u32[]{:S(2)}, u32[]{:S(2)}) collective-permute-start(f32[2,64]{1,0:T(2,128)} %get-tuple-element.8), channel_id=1, source_target_pairs={{0,1},{1,0},{2,3},{3,2},{4,5},{5,4},{6,7},{7,6},{8,9},{9,8},{10,11... | collective-permute-start | bytes 1544 | tf_op jit(solution)/shard_map/ppermute | solution.py:307
  49.0 3.6 %collective-permute-start.1 = (f32[2,64]{1,0:T(2,128)S(1)}, f32[2,64]{1,0:T(2,128)S(1)}, u32[]{:S(2)}, u32[]{:S(2)}) collective-permute-start(f32[2,64]{1,0:T(2,128)S(1)} %add.149), channel_id=1, source_target_pairs={{0,2},{1,3},{2,0},{3,1},{4,6},{5,7},{6,4},{7,5},{8,10},{9,11},{10,... | collective-permute-start | bytes 1544 | tf_op jit(solution)/shard_map/ppermute | solution.py:307
  52.6 5.1 %collective-permute-start.2 = (f32[2,64]{1,0:T(2,128)S(1)}, f32[2,64]{1,0:T(2,128)S(1)}, u32[]{:S(2)}, u32[]{:S(2)}) collective-permute-start(f32[2,64]{1,0:T(2,128)S(1)} %add.150), channel_id=1, source_target_pairs={{0,4},{1,5},{2,6},{3,7},{4,0},{5,1},{6,2},{7,3},{8,12},{9,13},{10,... | collective-permute-start | bytes 1544 | tf_op jit(solution)/shard_map/ppermute | solution.py:307
  57.7 5.3 %collective-permute-start.3 = (f32[2,64]{1,0:T(2,128)S(1)}, f32[2,64]{1,0:T(2,128)S(1)}, u32[]{:S(2)}, u32[]{:S(2)}) collective-permute-start(f32[2,64]{1,0:T(2,128)S(1)} %add.151), channel_id=1, source_target_pairs={{0,8},{1,9},{2,10},{3,11},{4,12},{5,13},{6,14},{7,15},{8,0},{9,1},... | collective-permute-start | bytes 1544 | tf_op jit(solution)/shard_map/ppermute | solution.py:307

commit v3 on v2

v3 whole, which is shorter than its diff:
```python
import functools

import jax
import jax.numpy as jnp
from jax import lax
from jax.experimental import pallas as pl
from jax.experimental.pallas import tpu as pltpu
from jax.sharding import PartitionSpec as P

LOOK = 9
RIM = LOOK // 2
LAGS = 4
SUB = 8
LANES = 128
EDGE = 2 * RIM
HALF = LANES // EDGE

F32 = jnp.float32
BF16 = jnp.bfloat16


def iota2(shape, dim):
    return lax.broadcasted_iota(jnp.int32, shape, dim)


def split2(value):
    high = value.astype(BF16)
    low = (value - high.astype(F32)).astype(BF16)
    return high, low


def window_rows(rows, count):
    def add(a, b):
        return b if a is None else (a if b is None else a + b)

    def at(series, i):
        return series.get(i)

    base = {i: rows[i] for i in range(count)}
    two = {i: add(at(base, i), at(base, i + 1)) for i in range(-RIM, count)}
    four = {i: add(at(two, i), at(two, i + 2)) for i in range(-RIM, count)}
    eight = {i: add(at(four, i), at(four, i + 4)) for i in range(-RIM, count)}
    return [add(at(eight, r - RIM), at(base, r + RIM)) for r in range(count)]


def column_band():
    source = lax.rem(iota2((2 * LANES, LANES), 0), LANES)
    return (jnp.abs(source - iota2((2 * LANES, LANES), 1)) <= RIM).astype(BF16)


def edge_matrix(row_count):
    size = row_count * EDGE
    source, target = iota2((size, size), 0), iota2((size, size), 1)
    near = jnp.abs(source // EDGE - target // EDGE) <= RIM
    e, t = source % EDGE, target % EDGE
    left = (e < RIM) & (t >= RIM) & (e >= t - RIM)
    right = (e >= RIM) & (t < RIM) & (t >= e - RIM)
    return (near & (left | right)).astype(BF16)


def observe_kernel(
    row_count, unit_count,
    group_ref, weight_ref, edge_weight_ref, band_ref, edge_ref, solve_ref, coord_ref,
    series_ref, sums_ref,
    re_s, im_s, wre_s, wim_s, pw_s, hre_s, him_s, hwre_s, hwim_s, obs_s,
):
    group = pl.program_id(0)
    slots = (unit_count + 1) * SUB
    halves = row_count // HALF
    per_unit, block_rows, _ = group_ref.shape
    date_dev = SUB // per_unit
    hbase = 2 * date_dev * row_count
    new = pl.multiple_of(group * SUB, SUB)

    for s in range(per_unit):
        for d in range(date_dev):
            for c, dst in ((0, re_s), (1, im_s)):
                start = (d * 2 + c) * row_count
                values = group_ref[s, pl.ds(start, row_count), :].astype(F32)
                for g in range(row_count // SUB):
                    at = pl.ds(g * SUB * slots + new + s * date_dev + d, SUB, stride=slots)
                    dst[at, :] = values[g * SUB : (g + 1) * SUB]
        edge = group_ref[s, pl.ds(hbase, 2 * halves * date_dev), :].astype(F32)
        for c, dst in ((0, hre_s), (1, him_s)):
            for h in range(halves):
                start = (c * halves + h) * date_dev
                dst[pl.ds(h * slots + new + s * date_dev, date_dev), :] = edge[start : start + date_dev]

    lane = iota2((SUB, LANES), 1)
    at_edge = (lane >= LANES - RIM) | (lane < RIM)

    def power(re, im, wre, wim, weights, count):
        out = []
        for r in range(count):
            at = pl.ds(r * slots + new, SUB)
            w = weights[pl.ds(r, 1), :]
            a_re, a_im = re[at, :], im[at, :]
            w_re, w_im = w * a_re, w * a_im
            wre[at, :] = w_re
            wim[at, :] = w_im
            out.append(w_re * a_re + w_im * a_im)
        return out

    def cross(re, im, wre, wim, count, lag, old):
        out = []
        for r in range(count):
            at, ahead = pl.ds(r * slots + old, SUB), pl.ds(r * slots + old + lag, SUB)
            out.append(wim[at, :] * re[ahead, :] - wre[at, :] * im[ahead, :])
        return out

    def at_edges(images):
        halo = jnp.concatenate([jnp.concatenate(image, axis=1) for image in images], axis=0)
        summed = jnp.dot(jnp.concatenate(split2(halo), axis=0), edge_ref[...], preferred_element_type=F32)
        return summed[: halo.shape[0]] + summed[halo.shape[0] :]

    def look(image, edges):
        rows = jnp.concatenate(window_rows(image, row_count), axis=0)
        summed = jnp.dot(jnp.concatenate(split2(rows), axis=1), band_ref[...], preferred_element_type=F32)
        out = []
        for r in range(row_count):
            tile = edges[:, (r // HALF) * LANES : (r // HALF + 1) * LANES]
            rolled = pltpu.roll(tile, (LANES - RIM - EDGE * (r % HALF)) % LANES, 1)
            out.append(summed[r * SUB : (r + 1) * SUB] + jnp.where(at_edge, rolled, 0.0))
        return out

    edges = at_edges([power(hre_s, him_s, hwre_s, hwim_s, edge_weight_ref, halves)])
    for r, value in enumerate(look(power(re_s, im_s, wre_s, wim_s, weight_ref, row_count), edges)):
        pw_s[pl.ds(r * slots + new, SUB), :] = value

    combos = unit_count * SUB * LAGS

    @pl.when(group > 0)
    def _():
        unit = group - 1
        old = pl.multiple_of(unit * SUB, SUB)
        lags = range(1, LAGS + 1)
        edges = at_edges([cross(hre_s, him_s, hwre_s, hwim_s, halves, lag, old) for lag in lags])

        def observed(lag):
            image = cross(re_s, im_s, wre_s, wim_s, row_count, lag, old)
            out = []
            for r, value in enumerate(look(image, edges[(lag - 1) * SUB : lag * SUB])):
                p = pw_s[pl.ds(r * slots + old, SUB), :]
                q = pw_s[pl.ds(r * slots + old + lag, SUB), :]
                out.append(value * lax.rsqrt(p * q + 1e-06))
            return out

        for lag in range(1, LAGS + 1, 2):
            first, second = observed(lag), observed(lag + 1)
            for r in range(row_count):
                at = pl.multiple_of(r * combos + unit * (SUB * LAGS) + (lag - 1) * SUB, 2 * SUB)
                obs_s[pl.ds(at, 2 * SUB), :] = jnp.concatenate([first[r], second[r]], axis=0).astype(BF16)

    @pl.when(group == unit_count)
    def _():
        solve = solve_ref[...]
        date_total = solve.shape[0] // 2
        mean = jnp.zeros((date_total, LANES), F32)
        for r in range(row_count):
            both = jnp.dot(solve, obs_s[pl.ds(r * combos, combos), :], preferred_element_type=F32)
            series = both[:date_total] + both[date_total:]
            for g in range(date_total // SUB):
                series_ref[pl.ds(g * SUB * row_count + r, SUB, stride=row_count), :] = series[g * SUB : (g + 1) * SUB]
            mean = mean + series
        eye = iota2((date_total, date_total), 0) == iota2((date_total, date_total), 1)
        for i, part in enumerate((mean, mean * coord_ref[...])):
            column = jnp.sum(part, axis=1, keepdims=True)
            sums_ref[pl.ds(i, 1), :] = jnp.sum(jnp.where(eye, column, 0.0), axis=0, keepdims=True)


def observe_all(blocks, weight, edge_weight, solve, coord, row_count, date_dev):
    per_unit = SUB // date_dev
    sources, block_rows, _ = blocks.shape
    unit_count = sources // per_unit
    date_total = unit_count * SUB
    combos = date_total * LAGS
    halves = row_count // HALF
    slots = (unit_count + 1) * SUB
    whole = lambda a: pl.BlockSpec(a.shape, lambda u: (0,) * a.ndim)
    band, edge = column_band(), edge_matrix(row_count)
    scratch = [pltpu.VMEM((row_count * slots, LANES), F32)] * 5
    scratch += [pltpu.VMEM((halves * slots, LANES), F32)] * 4
    scratch += [pltpu.VMEM((row_count * combos, LANES), BF16)]
    words = row_count * LANES * (5 * slots + combos // 2 + 2 * date_total) + date_total * LANES * combos // 64
    return pl.pallas_call(
        functools.partial(observe_kernel, row_count, unit_count),
        grid=(unit_count + 1,),
        out_shape=(
            jax.ShapeDtypeStruct((date_total * row_count, LANES), F32),
            jax.ShapeDtypeStruct((2, date_total), F32),
        ),
        in_specs=[
            pl.BlockSpec((per_unit, block_rows, LANES), lambda u: (lax.rem(u, unit_count), 0, 0)),
            whole(weight), whole(edge_weight), whole(band), whole(edge), whole(solve), whole(coord),
        ],
        out_specs=(
            pl.BlockSpec((date_total * row_count, LANES), lambda u: (0, 0)),
            pl.BlockSpec((2, date_total), lambda u: (0, 0)),
        ),
        scratch_shapes=scratch,
        compiler_params=pltpu.CompilerParams(
            dimension_semantics=("arbitrary",), vmem_limit_bytes=min(4 * words + 2**23, 2**26 - 2**17)
        ),
        name="observe",
    )(blocks, weight, edge_weight, band, edge, solve, coord)


def pack_kernel(date_dev, row_count, tiles_ref, out_ref, copies_s):
    strips = out_ref.shape[0]
    size = tiles_ref.shape[0]
    halves = row_count // HALF
    source, lane = iota2((2 * LANES, LANES), 0), iota2((2 * LANES, LANES), 1) % EDGE
    spread = (lane == jnp.where(source < LANES, source - (LANES - RIM), source - LANES + RIM)) & (
        (source >= LANES) == (lane >= RIM)
    )
    spread = spread.astype(BF16)
    mask = iota2((size, LANES), 0) % HALF == iota2((size, LANES), 1) // EDGE
    out_rows = 2 * halves * date_dev
    target, row = iota2((out_rows, size), 0), iota2((out_rows, size), 1)
    same = (
        (target % date_dev == row // (2 * row_count))
        & (target // (halves * date_dev) == row // row_count % 2)
        & (target // date_dev % halves == row // HALF % halves)
    ).astype(BF16)
    nothing = jnp.zeros((size, LANES), BF16)
    for j in range(strips):
        before = tiles_ref[:, (j - 1) * LANES : j * LANES] if j else nothing
        after = tiles_ref[:, (j + 1) * LANES : (j + 2) * LANES] if j + 1 < strips else nothing
        copies = jnp.dot(jnp.concatenate([before, after], axis=1), spread, preferred_element_type=F32)
        copies_s[:, j * LANES : (j + 1) * LANES] = jnp.where(mask, copies, 0.0).astype(BF16)
    for j in range(strips):
        out_ref[j, pl.ds(0, size), :] = tiles_ref[:, j * LANES : (j + 1) * LANES]
    edge = jnp.dot(same, copies_s[...], preferred_element_type=F32).astype(BF16)
    for j in range(strips):
        out_ref[j, pl.ds(size, out_rows), :] = edge[:, j * LANES : (j + 1) * LANES]


def pack(tiles, devices):
    date_dev, _, row_count, col_total = tiles.shape
    size = date_dev * 2 * row_count
    block_rows = size + 2 * (row_count // HALF) * date_dev
    return pl.pallas_call(
        functools.partial(pack_kernel, date_dev, row_count),
        out_shape=jax.ShapeDtypeStruct((devices, block_rows, LANES), BF16),
        in_specs=[pl.BlockSpec(memory_space=pltpu.VMEM)],
        out_specs=pl.BlockSpec(memory_space=pltpu.VMEM),
        scratch_shapes=[pltpu.VMEM((size, col_total), BF16)],
        compiler_params=pltpu.CompilerParams(vmem_limit_bytes=8 * size * col_total + 2**22),
        name="pack",
    )(tiles.reshape(size, col_total))


def remove_kernel(pixels, square_sum, series_ref, sums_ref, more_ref, coord_ref, out_ref, out_s, sems):
    dates = sums_ref.shape[1]
    eye = iota2((dates, dates), 0) == iota2((dates, dates), 1)
    sums = sums_ref[...]
    for i in range(more_ref.shape[0]):
        sums = sums + more_ref[i]
    mean = jnp.sum(jnp.where(eye, sums[0:1], 0.0), axis=1, keepdims=True) / pixels
    slope = jnp.sum(jnp.where(eye, sums[1:2], 0.0), axis=1, keepdims=True) / square_sum
    trend = mean + slope * coord_ref[...]
    rows = series_ref.shape[0] // dates
    chunks = sems.shape[0]
    per_chunk = dates // chunks
    copies = []
    for i in range(chunks):
        for d in range(i * per_chunk, (i + 1) * per_chunk):
            at = pl.ds(d * rows, rows)
            out_s[at, :] = series_ref[at, :] - trend[d : d + 1]
        at = pl.ds(i * per_chunk * rows, per_chunk * rows)
        copies.append(pltpu.make_async_copy(out_s.at[at], out_ref.at[at], sems.at[i]))
        copies[-1].start()
    for copy in copies:
        copy.wait()


def remove_trend(series, sums, more, coord, pixels, square_sum):
    chunks = 8
    return pl.pallas_call(
        functools.partial(remove_kernel, pixels, square_sum),
        out_shape=jax.ShapeDtypeStruct(series.shape, F32),
        in_specs=[pl.BlockSpec(memory_space=pltpu.VMEM)] * 4,
        out_specs=pl.BlockSpec(memory_space=pl.ANY),
        scratch_shapes=[pltpu.VMEM(series.shape, F32), pltpu.SemaphoreType.DMA((chunks,))],
        compiler_params=pltpu.CompilerParams(vmem_limit_bytes=8 * series.size + 2**22),
        name="remove",
    )(series, sums, more, coord)


def solve_matrix(pair_list, date_total):
    first, lag = pair_list[:, 0], pair_list[:, 1] - pair_list[:, 0]
    dates = lax.iota(jnp.int32, date_total)
    at_first = (dates[:, None] == first[None, :]).astype(F32)
    at_second = (dates[:, None] == pair_list[None, :, 1]).astype(F32)
    incidence = (at_first - at_second).astype(BF16)
    normal_matrix = jnp.dot(incidence, incidence.T, preferred_element_type=F32) + jnp.eye(date_total, dtype=F32)
    factor = jnp.linalg.cholesky(normal_matrix)
    lags = lax.iota(jnp.int32, LAGS) + 1
    at_lag = (lags[:, None] == lag[None, :]).astype(BF16)
    count = jnp.dot(at_lag, at_first.astype(BF16).T, preferred_element_type=F32)
    second = dates[None, :] + lags[:, None]
    ends = (dates[:, None, None] == dates[None, None, :]).astype(F32) - (
        dates[:, None, None] == second[None]
    ).astype(F32)
    columns = ends * count[None]
    units = date_total // SUB
    columns = columns.reshape(date_total, LAGS, units, SUB).transpose(0, 2, 1, 3).reshape(date_total, LAGS * date_total)
    solved = jax.scipy.linalg.cho_solve((factor, True), columns)
    return jnp.concatenate(split2(solved), axis=0)


def body(slc_tiles, look_weight, pair_list):
    devices = lax.axis_size("gx")
    position = lax.axis_index("gx")
    date_dev, _, row_count, col_total = slc_tiles.shape
    strip = col_total // devices
    date_total = date_dev * devices
    halves = row_count // HALF

    blocks = lax.all_to_all(pack(slc_tiles, devices), "gx", 0, 0, tiled=True)

    weight = lax.dynamic_slice_in_dim(look_weight, position * strip, strip, 1)
    weight_pad = jnp.pad(look_weight, ((0, 0), (RIM, RIM)))
    edge_weight = jnp.concatenate(
        [
            lax.dynamic_slice_in_dim(weight_pad, position * strip, RIM, 1),
            lax.dynamic_slice_in_dim(weight_pad, position * strip + strip + RIM, RIM, 1),
        ],
        axis=1,
    ).reshape(halves, LANES)
    solve = solve_matrix(pair_list, date_total)
    column_ids = position * strip + lax.iota(jnp.int32, strip)
    columns = (2.0 * column_ids.astype(F32) + 1.0) / col_total - 1.0

    series, sums = observe_all(blocks, weight, edge_weight, solve, columns[None], row_count, date_dev)
    rounds = []
    step = devices
    while step > 1:
        width = 4 if step % 4 == 0 else 2
        step //= width
        rounds.append([step * k for k in range(1, width)])
    for i, round_ in enumerate(rounds):
        parts = [lax.ppermute(sums, "gx", [(s, s ^ k) for s in range(devices)]) for k in round_]
        if i + 1 < len(rounds):
            for part in parts:
                sums = sums + part
    square_sum = row_count * (col_total * col_total - 1) / (3 * col_total)
    out = remove_trend(series, sums, jnp.stack(parts), columns[None], float(row_count * col_total), square_sum)
    return out.reshape(date_total, row_count, strip)


def solution(mesh):
    return jax.shard_map(
        body,
        mesh=mesh,
        in_specs=(P("gx", None, "band", None), P("band", None), P()),
        out_specs=P(None, "band", "gx"),
        check_vma=False,
    )
```

time: 68.1 us -> 56.1 us (0.82)
  Pallas kernels: 18.1 us -> 10 us
  waiting for transfers between devices: 9.97 us -> 14.5 us
  other arithmetic: 17.2 us -> 12.8 us
  starting transfers between devices: 17.4 us -> 15.5 us
  local copies, waits for them, and re-layouts: 3.44 us -> 1.94 us
    all_to_all x1, waiting for transfers between devices: 5.84 us -> 9.43 us  [body(): blocks = lax.all_to_all(pack(slc_tiles, devices), 'gx', 0, 0, tiled=True)]
    pallas_call x1, Pallas kernels: 4.11 us -> 1.12 us  [remove_trend(): pl.pallas_call(functools.partial(remove_kernel, pixels, square_sum), out_...]
    pallas_call x1, Pallas kernels: 4.64 us -> 1.89 us  [pack(): pl.pallas_call(functools.partial(pack_kernel, date_dev, row_count), out_s...]
    pallas_call x1, Pallas kernels: 9.35 us -> 6.99 us  [observe_all(): pl.pallas_call(functools.partial(observe_kernel, row_count, unit_count),...]
    ppermute x4 -> x6, starting transfers between devices: 9.81 us -> 7.95 us  [body(): lax.ppermute(sums, 'gx', [(s, s ^ k) for s in range(devices)])]
    add x4 -> x1, other arithmetic: 1.25 us -> 0.01 us  [body(): sums = sums + part]
    ppermute x4 -> x6, waiting for transfers between devices: 4.13 us -> 5.11 us  [body(): lax.ppermute(sums, 'gx', [(s, s ^ k) for s in range(devices)])]
    unnamed x9 -> x7, local copies, waits for them, and re-layouts: 1.35 us -> 1.57 us
  transfers between devices with their start and end apart: 5 -> 7, of which waited for: 4 -> 5; matrix products, arithmetic and copies ran while one was open for 28% -> 26% of each run, Pallas kernels for 0% -> 0%
where the time goes in v3:
time: 56.1 us; the launch traced here: 55.8 us
  starting transfers between devices  15.5 us (28%)
  waiting for transfers between devices  14.5 us (26%)
  other arithmetic  12.8 us (23%)
  Pallas kernels  10 us (18%)
  local copies, waits for them, and re-layouts  1.94 us (3%)
  matrix products  0.81 us (1%)
    all_to_all x1, waiting for transfers between devices, body(): blocks = lax.all_to_all(pack(slc_tiles, devices), 'gx', 0, 0, tiled=True)  9.43 us
    ppermute x6, starting transfers between devices, body(): lax.ppermute(sums, 'gx', [(s, s ^ k) for s in range(devices)])  7.95 us
    all_to_all x1, starting transfers between devices, body(): blocks = lax.all_to_all(pack(slc_tiles, devices), 'gx', 0, 0, tiled=True)  7.55 us
    pallas_call x1, Pallas kernels, observe_all(): pl.pallas_call(functools.partial(observe_kernel, row_count, unit_count),...  6.99 us
    another operation x3, other arithmetic, solve_matrix(): factor = jnp.linalg.cholesky(normal_matrix)  6.52 us
    another operation x2, other arithmetic, solve_matrix(): solved = jax.scipy.linalg.cho_solve((factor, True), columns)  5.56 us
    ppermute x6, waiting for transfers between devices, body(): lax.ppermute(sums, 'gx', [(s, s ^ k) for s in range(devices)])  5.11 us
    pallas_call x1, Pallas kernels, pack(): pl.pallas_call(functools.partial(pack_kernel, date_dev, row_count), out_s...  1.89 us
  transfers between devices with their start and end apart: 7, of which 5 were waited for; matrix products, arithmetic and copies ran while one was open for 26% of the time, Pallas kernels for 0%

profile of v3, /device:TPU:0, one launch (start us, length us, event | category | flops | bytes accessed | tf_op | source)
XLA Modules:
  0.0 55.8 jit_solution(17110665740073661640)
XLA Ops:
  0.0 1.2 %copy-done = bf16[4,2,32,2048]{3,2,1,0:T(8,128)(2,1)S(1)} copy-done((bf16[4,2,32,2048]{3,2,1,0:T(8,128)(2,1)S(1)}, bf16[4,2,32,2048]{3,2,1,0:T(8,128)(2,1)}, u32[]{:S(2)}) %copy-start) | copy-done | bytes 1048600
  1.2 1.9 %pack.1 = bf16[16,272,128]{2,1,0:T(8,128)(2,1)} custom-call(bf16[256,2048]{1,0:T(8,128)(2,1)S(1)} %bitcast.26), custom_call_target="tpu_custom_call" | custom-call | tf_op jit(solution)/shard_map/pack/pallas_call | solution.py:242
  3.1 7.5 %all-to-all-start = ((bf16[16,272,128]{2,1,0:T(8,128)(2,1)}), bf16[16,272,128]{2,1,0:T(8,128)(2,1)S(1)}, u32[]{:S(2)}, u32[]{:S(2)}) async-start(bf16[16,272,128]{2,1,0:T(8,128)(2,1)} %pack.1), calls=%async_computation | async-start | bytes 2228224 | tf_op jit(solution)/shard_map/all_to_all | solution.py:320
  10.9 0.3 copy.8
  11.4 5.8 %cholesky.17 = f32[64,64]{1,0:T(8,128)S(1)} custom-call(f32[64,64]{1,0:T(8,128)S(1)} %fusion.18), custom_call_target="Cholesky" | custom-call | tf_op jit(solution)/shard_map/jit(cholesky)/cholesky | solution.py:297
  17.2 0.6 %compare_reduce_fusion = pred[]{:T(512)} fusion(f32[64]{0:T(128)S(1)} %select_reduce_fusion), kind=kLoop, calls=%fused_computation.59 | loop fusion | flops 127 | bytes 257 | tf_op jit(solution)/shard_map/jit(cholesky)/cholesky | solution.py:297
  17.9 0.7 %fusion.9 = f32[1,64,64]{2,1,0:T(8,128)S(1)} fusion(f32[64,64]{1,0:T(8,128)S(1)} %cholesky.17, pred[]{:T(512)} %compare_reduce_fusion), kind=kLoop, calls=%fused_computation.30 | loop fusion | flops 16384 | bytes 32769 | tf_op jit(solution)/shard_map/jit(_cho_solve)/triangular_solve | solution.py:308
  18.6 0.2 fusion.12
  19.0 4.9 %custom-call.10 = f32[1,64,64]{1,2,0:T(8,128)S(1)} custom-call(f32[1,64,64]{2,1,0:T(8,128)S(1)} %fusion.9), custom_call_target="InvertDiagBlocksLowerTriangular" | custom-call | tf_op jit(solution)/shard_map/jit(_cho_solve)/triangular_solve | solution.py:308
  24.3 0.3 fusion.15
  24.6 0.2 subtract_convert_fusion
  24.9 0.3 fusion.3.edge_ref
  25.2 9.4 %all-to-all-done.group_ref = bf16[16,272,128]{2,1,0:T(8,128)(2,1)S(1)} async-done(((bf16[16,272,128]{2,1,0:T(8,128)(2,1)}), bf16[16,272,128]{2,1,0:T(8,128)(2,1)S(1)}, u32[]{:S(2)}, u32[]{:S(2)}) %all-to-all-start) | async-done | bytes 1114144 | tf_op jit(solution)/shard_map/all_to_all | solution.py:320
  34.6 7.0 %observe.1 = (f32[2048,128]{1,0:T(8,128)S(1)}, f32[2,64]{1,0:T(2,128)S(1)}) custom-call(bf16[16,272,128]{2,1,0:T(8,128)(2,1)S(1)} %all-to-all-done.group_ref, f32[32,128]{1,0:T(8,128)S(1)} %constant_dynamic-slice_fusion.weight_ref, f32[2,128]{1,0:T(2,128)S(1)} %reshape.150.edge_weight_ref, bf16[256,128]{1,0:T(8,128)(2,1)S(1)} %fusion.7.band_ref, ...), custom_call_target="tpu_custom_call" | custom-call | tf_op jit(solution)/shard_map/observe/pallas_call | solution.py:185
  41.6 3.4 %collective-permute-start.2 = (f32[2,64]{1,0:T(2,128)S(1)}, f32[2,64]{1,0:T(2,128)S(1)}, u32[]{:S(2)}, u32[]{:S(2)}) collective-permute-start(f32[2,64]{1,0:T(2,128)S(1)} %get-tuple-element.8), channel_id=1, source_target_pairs={{0,12},{1,13},{2,14},{3,15},{4,8},{5,9},{6,10},{7,11},{8,4},{9,5},... | collective-permute-start | bytes 1544 | tf_op jit(solution)/shard_map/ppermute | solution.py:343
  45.0 2.1 %collective-permute-start.1 = (f32[2,64]{1,0:T(2,128)S(1)}, f32[2,64]{1,0:T(2,128)S(1)}, u32[]{:S(2)}, u32[]{:S(2)}) collective-permute-start(f32[2,64]{1,0:T(2,128)S(1)} %get-tuple-element.8), channel_id=1, source_target_pairs={{0,8},{1,9},{2,10},{3,11},{4,12},{5,13},{6,14},{7,15},{8,0},{9,1},... | collective-permute-start | bytes 1544 | tf_op jit(solution)/shard_map/ppermute | solution.py:343
  47.2 0.5 collective-permute-start
  47.7 1.8 %collective-permute-done.1 = f32[2,64]{1,0:T(2,128)S(1)} collective-permute-done((f32[2,64]{1,0:T(2,128)S(1)}, f32[2,64]{1,0:T(2,128)S(1)}, u32[]{:S(2)}, u32[]{:S(2)}) %collective-permute-start.1) | collective-permute-done | bytes 544 | tf_op jit(solution)/shard_map/ppermute | solution.py:343
  49.5 1.2 %collective-permute-done = f32[2,64]{1,0:T(2,128)S(1)} collective-permute-done((f32[2,64]{1,0:T(2,128)S(1)}, f32[2,64]{1,0:T(2,128)S(1)}, u32[]{:S(2)}, u32[]{:S(2)}) %collective-permute-start) | collective-permute-done | bytes 544 | tf_op jit(solution)/shard_map/ppermute | solution.py:343
  50.8 0.3 collective-permute-start.5
  51.1 1.5 %collective-permute-start.4 = (f32[2,64]{1,0:T(2,128)S(1)}, f32[2,64]{1,0:T(2,128)S(1)}, u32[]{:S(2)}, u32[]{:S(2)}) collective-permute-start(f32[2,64]{1,0:T(2,128)S(1)} %add_add_fusion.sums_ref), channel_id=1, source_target_pairs={{0,2},{1,3},{2,0},{3,1},{4,6},{5,7},{6,4},{7,5},{8,10},{9,11},{10,... | collective-permute-start | bytes 1544 | tf_op jit(solution)/shard_map/ppermute | solution.py:343
  52.7 1.1 %collective-permute-done.5 = f32[2,64]{1,0:T(2,128)S(1)} collective-permute-done((f32[2,64]{1,0:T(2,128)S(1)}, f32[2,64]{1,0:T(2,128)S(1)}, u32[]{:S(2)}, u32[]{:S(2)}) %collective-permute-start.5) | collective-permute-done | bytes 544 | tf_op jit(solution)/shard_map/ppermute | solution.py:343
  53.8 0.9 %collective-permute-done.4 = f32[2,64]{1,0:T(2,128)S(1)} collective-permute-done((f32[2,64]{1,0:T(2,128)S(1)}, f32[2,64]{1,0:T(2,128)S(1)}, u32[]{:S(2)}, u32[]{:S(2)}) %collective-permute-start.4) | collective-permute-done | bytes 544 | tf_op jit(solution)/shard_map/ppermute | solution.py:343
  54.7 1.1 %remove.1 = f32[2048,128]{1,0:T(8,128)} custom-call(f32[2048,128]{1,0:T(8,128)S(1)} %get-tuple-element.7.series_ref, f32[2,64]{1,0:T(2,128)S(1)} %add_add_fusion.sums_ref, f32[3,2,64]{2,1,0:T(2,128)S(1)} %pad_maximum_fusion.2.more_ref, f32[1,128]{1,0:T(1,128)S(1)} %multiply_add_fusion.1.coord_ref), custom_call_target="tpu_custom_call" | custom-call | tf_op jit(solution)/shard_map/remove/pallas_call | solution.py:279
  (35 shorter events, 1.1 us)
Async XLA Ops:
  0.0 1.2 %copy-start = (bf16[4,2,32,2048]{3,2,1,0:T(8,128)(2,1)S(1)}, bf16[4,2,32,2048]{3,2,1,0:T(8,128)(2,1)}, u32[]{:S(2)}) copy-start(bf16[4,2,32,2048]{3,2,1,0:T(8,128)(2,1)} %param.3) | copy-start | bytes 3145732
  3.1 7.6 %copy-start.2 = (s32[192,2]{0,1:T(2,128)S(1)}, s32[192,2]{0,1:T(2,128)}, u32[]{:S(2)}) copy-start(s32[192,2]{0,1:T(2,128)} %param.5) | copy-start | bytes 4612
  3.1 7.8 %copy-start.1 = (f32[32,2048]{1,0:T(8,128)S(1)}, f32[32,2048]{1,0:T(8,128)}, u32[]{:S(2)}) copy-start(f32[32,2048]{1,0:T(8,128)} %param.4) | copy-start | bytes 786436
  3.1 31.5 %all-to-all-start = ((bf16[16,272,128]{2,1,0:T(8,128)(2,1)}), bf16[16,272,128]{2,1,0:T(8,128)(2,1)S(1)}, u32[]{:S(2)}, u32[]{:S(2)}) async-start(bf16[16,272,128]{2,1,0:T(8,128)(2,1)} %pack.1), calls=%async_computation | async-start | bytes 2228224 | tf_op jit(solution)/shard_map/all_to_all | solution.py:320
  41.6 6.1 %collective-permute-start.2 = (f32[2,64]{1,0:T(2,128)S(1)}, f32[2,64]{1,0:T(2,128)S(1)}, u32[]{:S(2)}, u32[]{:S(2)}) collective-permute-start(f32[2,64]{1,0:T(2,128)S(1)} %get-tuple-element.8), channel_id=1, source_target_pairs={{0,12},{1,13},{2,14},{3,15},{4,8},{5,9},{6,10},{7,11},{8,4},{9,5},... | collective-permute-start | bytes 1544 | tf_op jit(solution)/shard_map/ppermute | solution.py:343
  45.0 4.5 %collective-permute-start.1 = (f32[2,64]{1,0:T(2,128)S(1)}, f32[2,64]{1,0:T(2,128)S(1)}, u32[]{:S(2)}, u32[]{:S(2)}) collective-permute-start(f32[2,64]{1,0:T(2,128)S(1)} %get-tuple-element.8), channel_id=1, source_target_pairs={{0,8},{1,9},{2,10},{3,11},{4,12},{5,13},{6,14},{7,15},{8,0},{9,1},... | collective-permute-start | bytes 1544 | tf_op jit(solution)/shard_map/ppermute | solution.py:343
  47.2 3.6 %collective-permute-start = (f32[2,64]{1,0:T(2,128)S(1)}, f32[2,64]{1,0:T(2,128)S(1)}, u32[]{:S(2)}, u32[]{:S(2)}) collective-permute-start(f32[2,64]{1,0:T(2,128)S(1)} %get-tuple-element.8), channel_id=1, source_target_pairs={{0,4},{1,5},{2,6},{3,7},{4,0},{5,1},{6,2},{7,3},{8,12},{9,13},{10,... | collective-permute-start | bytes 1544 | tf_op jit(solution)/shard_map/ppermute | solution.py:343
  50.8 3.0 %collective-permute-start.5 = (f32[2,64]{1,0:T(2,128)S(1)}, f32[2,64]{1,0:T(2,128)S(1)}, u32[]{:S(2)}, u32[]{:S(2)}) collective-permute-start(f32[2,64]{1,0:T(2,128)S(1)} %add_add_fusion.sums_ref), channel_id=1, source_target_pairs={{0,3},{1,2},{2,1},{3,0},{4,7},{5,6},{6,5},{7,4},{8,11},{9,10},{10,... | collective-permute-start | bytes 1544 | tf_op jit(solution)/shard_map/ppermute | solution.py:343
  51.1 3.6 %collective-permute-start.4 = (f32[2,64]{1,0:T(2,128)S(1)}, f32[2,64]{1,0:T(2,128)S(1)}, u32[]{:S(2)}, u32[]{:S(2)}) collective-permute-start(f32[2,64]{1,0:T(2,128)S(1)} %add_add_fusion.sums_ref), channel_id=1, source_target_pairs={{0,2},{1,3},{2,0},{3,1},{4,6},{5,7},{6,4},{7,5},{8,10},{9,11},{10,... | collective-permute-start | bytes 1544 | tf_op jit(solution)/shard_map/ppermute | solution.py:343
  52.6 2.1 %collective-permute-start.3 = (f32[2,64]{1,0:T(2,128)S(1)}, f32[2,64]{1,0:T(2,128)S(1)}, u32[]{:S(2)}, u32[]{:S(2)}) collective-permute-start(f32[2,64]{1,0:T(2,128)S(1)} %add_add_fusion.sums_ref), channel_id=1, source_target_pairs={{0,1},{1,0},{2,3},{3,2},{4,5},{5,4},{6,7},{7,6},{8,9},{9,8},{10,11... | collective-permute-start | bytes 1544 | tf_op jit(solution)/shard_map/ppermute | solution.py:343

commit v4 on v3

--- a/solution.py
+++ b/solution.py
@@ -60,36 +60,37 @@
 
 def observe_kernel(
     row_count, unit_count,
-    group_ref, weight_ref, edge_weight_ref, band_ref, edge_ref, solve_ref, coord_ref,
+    first_ref, next_ref, weight_ref, edge_weight_ref, band_ref, edge_ref, solve_ref, coord_ref,
     series_ref, sums_ref,
     re_s, im_s, wre_s, wim_s, pw_s, hre_s, him_s, hwre_s, hwim_s, obs_s,
 ):
-    group = pl.program_id(0)
+    unit = pl.program_id(0)
     slots = (unit_count + 1) * SUB
     halves = row_count // HALF
-    per_unit, block_rows, _ = group_ref.shape
+    per_unit, block_rows, _ = next_ref.shape
     date_dev = SUB // per_unit
     hbase = 2 * date_dev * row_count
-    new = pl.multiple_of(group * SUB, SUB)
-
-    for s in range(per_unit):
-        for d in range(date_dev):
-            for c, dst in ((0, re_s), (1, im_s)):
-                start = (d * 2 + c) * row_count
-                values = group_ref[s, pl.ds(start, row_count), :].astype(F32)
-                for g in range(row_count // SUB):
-                    at = pl.ds(g * SUB * slots + new + s * date_dev + d, SUB, stride=slots)
-                    dst[at, :] = values[g * SUB : (g + 1) * SUB]
-        edge = group_ref[s, pl.ds(hbase, 2 * halves * date_dev), :].astype(F32)
-        for c, dst in ((0, hre_s), (1, him_s)):
-            for h in range(halves):
-                start = (c * halves + h) * date_dev
-                dst[pl.ds(h * slots + new + s * date_dev, date_dev), :] = edge[start : start + date_dev]
+    pad = series_ref.shape[0] // solve_ref.shape[0] * 2
+
+    def place(group_ref, new):
+        for s in range(per_unit):
+            for d in range(date_dev):
+                for c, dst in ((0, re_s), (1, im_s)):
+                    start = (d * 2 + c) * row_count
+                    values = group_ref[s, pl.ds(start, row_count), :].astype(F32)
+                    for g in range(row_count // SUB):
+                        at = pl.ds(g * SUB * slots + new + s * date_dev + d, SUB, stride=slots)
+                        dst[at, :] = values[g * SUB : (g + 1) * SUB]
+            edge = group_ref[s, pl.ds(hbase, 2 * halves * date_dev), :].astype(F32)
+            for c, dst in ((0, hre_s), (1, him_s)):
+                for h in range(halves):
+                    start = (c * halves + h) * date_dev
+                    dst[pl.ds(h * slots + new + s * date_dev, date_dev), :] = edge[start : start + date_dev]
 
     lane = iota2((SUB, LANES), 1)
     at_edge = (lane >= LANES - RIM) | (lane < RIM)
 
-    def power(re, im, wre, wim, weights, count):
+    def power(re, im, wre, wim, weights, count, new):
         out = []
         for r in range(count):
             at = pl.ds(r * slots + new, SUB)
@@ -123,45 +124,56 @@
             out.append(summed[r * SUB : (r + 1) * SUB] + jnp.where(at_edge, rolled, 0.0))
         return out
 
-    edges = at_edges([power(hre_s, him_s, hwre_s, hwim_s, edge_weight_ref, halves)])
-    for r, value in enumerate(look(power(re_s, im_s, wre_s, wim_s, weight_ref, row_count), edges)):
-        pw_s[pl.ds(r * slots + new, SUB), :] = value
+    def bring(group_ref, new):
+        place(group_ref, new)
+        edges = at_edges([power(hre_s, him_s, hwre_s, hwim_s, edge_weight_ref, halves, new)])
+        image = power(re_s, im_s, wre_s, wim_s, weight_ref, row_count, new)
+        for r, value in enumerate(look(image, edges)):
+            pw_s[pl.ds(r * slots + new, SUB), :] = value
 
     combos = unit_count * SUB * LAGS
 
-    @pl.when(group > 0)
+    @pl.when(unit == 0)
     def _():
-        unit = group - 1
-        old = pl.multiple_of(unit * SUB, SUB)
-        lags = range(1, LAGS + 1)
-        edges = at_edges([cross(hre_s, him_s, hwre_s, hwim_s, halves, lag, old) for lag in lags])
-
-        def observed(lag):
-            image = cross(re_s, im_s, wre_s, wim_s, row_count, lag, old)
-            out = []
-            for r, value in enumerate(look(image, edges[(lag - 1) * SUB : lag * SUB])):
-                p = pw_s[pl.ds(r * slots + old, SUB), :]
-                q = pw_s[pl.ds(r * slots + old + lag, SUB), :]
-                out.append(value * lax.rsqrt(p * q + 1e-06))
-            return out
-
-        for lag in range(1, LAGS + 1, 2):
-            first, second = observed(lag), observed(lag + 1)
-            for r in range(row_count):
-                at = pl.multiple_of(r * combos + unit * (SUB * LAGS) + (lag - 1) * SUB, 2 * SUB)
-                obs_s[pl.ds(at, 2 * SUB), :] = jnp.concatenate([first[r], second[r]], axis=0).astype(BF16)
-
-    @pl.when(group == unit_count)
+        bring(first_ref, pl.multiple_of(unit * SUB, SUB))
+
+    old = pl.multiple_of(unit * SUB, SUB)
+    @pl.when(unit < unit_count)
+    def _():
+        bring(next_ref, pl.multiple_of(old + SUB, SUB))
+
+    edges = at_edges([cross(hre_s, him_s, hwre_s, hwim_s, halves, lag, old) for lag in range(1, LAGS + 1)])
+
+    def observed(lag):
+        image = cross(re_s, im_s, wre_s, wim_s, row_count, lag, old)
+        out = []
+        for r, value in enumerate(look(image, edges[(lag - 1) * SUB : lag * SUB])):
+            p = pw_s[pl.ds(r * slots + old, SUB), :]
+            q = pw_s[pl.ds(r * slots + old + lag, SUB), :]
+            out.append(value * lax.rsqrt(p * q + 1e-06))
+        return out
+
+    for lag in range(1, LAGS + 1, 2):
+        first, second = observed(lag), observed(lag + 1)
+        for r in range(row_count):
+            at = pl.multiple_of(r * combos + unit * (SUB * LAGS) + (lag - 1) * SUB, 2 * SUB)
+            obs_s[pl.ds(at, 2 * SUB), :] = jnp.concatenate([first[r], second[r]], axis=0).astype(BF16)
+
+    @pl.when(unit == unit_count - 1)
     def _():
         solve = solve_ref[...]
         date_total = solve.shape[0] // 2
         mean = jnp.zeros((date_total, LANES), F32)
-        for r in range(row_count):
-            both = jnp.dot(solve, obs_s[pl.ds(r * combos, combos), :], preferred_element_type=F32)
-            series = both[:date_total] + both[date_total:]
-            for g in range(date_total // SUB):
-                series_ref[pl.ds(g * SUB * row_count + r, SUB, stride=row_count), :] = series[g * SUB : (g + 1) * SUB]
-            mean = mean + series
+        for r in range(0, row_count, 2):
+            pair = [obs_s[pl.ds((r + i) * combos, combos), :] for i in range(2)]
+            both = jnp.dot(solve, jnp.concatenate(pair, axis=1), preferred_element_type=F32)
+            both = both[:date_total] + both[date_total:]
+            for i in range(2):
+                series = both[:, i * LANES : (i + 1) * LANES]
+                for g in range(date_total // SUB):
+                    at = pl.ds(g * SUB * pad + r + i, SUB, stride=pad)
+                    series_ref[at, :] = series[g * SUB : (g + 1) * SUB]
+                mean = mean + series
         eye = iota2((date_total, date_total), 0) == iota2((date_total, date_total), 1)
         for i, part in enumerate((mean, mean * coord_ref[...])):
             column = jnp.sum(part, axis=1, keepdims=True)
@@ -176,25 +188,27 @@
     combos = date_total * LAGS
     halves = row_count // HALF
     slots = (unit_count + 1) * SUB
+    pad = row_count + SUB
     whole = lambda a: pl.BlockSpec(a.shape, lambda u: (0,) * a.ndim)
     band, edge = column_band(), edge_matrix(row_count)
     scratch = [pltpu.VMEM((row_count * slots, LANES), F32)] * 5
     scratch += [pltpu.VMEM((halves * slots, LANES), F32)] * 4
     scratch += [pltpu.VMEM((row_count * combos, LANES), BF16)]
-    words = row_count * LANES * (5 * slots + combos // 2 + 2 * date_total) + date_total * LANES * combos // 64
+    words = row_count * LANES * (5 * slots + combos // 2 + 3 * date_total) + date_total * LANES * combos // 64
     return pl.pallas_call(
         functools.partial(observe_kernel, row_count, unit_count),
-        grid=(unit_count + 1,),
+        grid=(unit_count,),
         out_shape=(
-            jax.ShapeDtypeStruct((date_total * row_count, LANES), F32),
+            jax.ShapeDtypeStruct((date_total * pad, LANES), F32),
             jax.ShapeDtypeStruct((2, date_total), F32),
         ),
         in_specs=[
-            pl.BlockSpec((per_unit, block_rows, LANES), lambda u: (lax.rem(u, unit_count), 0, 0)),
+            pl.BlockSpec((per_unit, block_rows, LANES), lambda u: (0, 0, 0)),
+            pl.BlockSpec((per_unit, block_rows, LANES), lambda u: (lax.rem(u + 1, unit_count), 0, 0)),
             whole(weight), whole(edge_weight), whole(band), whole(edge), whole(solve), whole(coord),
         ],
         out_specs=(
-            pl.BlockSpec((date_total * row_count, LANES), lambda u: (0, 0)),
+            pl.BlockSpec((date_total * pad, LANES), lambda u: (0, 0)),
             pl.BlockSpec((2, date_total), lambda u: (0, 0)),
         ),
         scratch_shapes=scratch,
@@ -202,13 +216,20 @@
             dimension_semantics=("arbitrary",), vmem_limit_bytes=min(4 * words + 2**23, 2**26 - 2**17)
         ),
         name="observe",
-    )(blocks, weight, edge_weight, band, edge, solve, coord)
-
-
-def pack_kernel(date_dev, row_count, tiles_ref, out_ref, copies_s):
+    )(blocks, blocks, weight, edge_weight, band, edge, solve, coord)
+
+
+def pack_kernel(date_dev, row_count, tiles_ref, out_ref, tiles_s, copies_s, edge_s, in_sems, out_sems, edge_sem):
     strips = out_ref.shape[0]
-    size = tiles_ref.shape[0]
+    size, col_total = tiles_s.shape
     halves = row_count // HALF
+    chunks = in_sems.shape[0]
+    per_chunk = strips // chunks
+    arrivals = []
+    for i in range(chunks):
+        at = pl.ds(i * per_chunk * LANES, per_chunk * LANES)
+        arrivals.append(pltpu.make_async_copy(tiles_ref.at[:, at], tiles_s.at[:, at], in_sems.at[i]))
+        arrivals[-1].start()
     source, lane = iota2((2 * LANES, LANES), 0), iota2((2 * LANES, LANES), 1) % EDGE
     spread = (lane == jnp.where(source < LANES, source - (LANES - RIM), source - LANES + RIM)) & (
         (source >= LANES) == (lane >= RIM)
@@ -223,16 +244,29 @@
         & (target // date_dev % halves == row // HALF % halves)
     ).astype(BF16)
     nothing = jnp.zeros((size, LANES), BF16)
-    for j in range(strips):
-        before = tiles_ref[:, (j - 1) * LANES : j * LANES] if j else nothing
-        after = tiles_ref[:, (j + 1) * LANES : (j + 2) * LANES] if j + 1 < strips else nothing
-        copies = jnp.dot(jnp.concatenate([before, after], axis=1), spread, preferred_element_type=F32)
-        copies_s[:, j * LANES : (j + 1) * LANES] = jnp.where(mask, copies, 0.0).astype(BF16)
-    for j in range(strips):
-        out_ref[j, pl.ds(0, size), :] = tiles_ref[:, j * LANES : (j + 1) * LANES]
+    departures = []
+    done = 0
+    for i in range(chunks):
+        arrivals[i].wait()
+        ready = (i + 1) * per_chunk
+        for j in range(ready - per_chunk, ready):
+            strip = tiles_s.at[:, pl.ds(j * LANES, LANES)]
+            departures.append(pltpu.make_async_copy(strip, out_ref.at[j, pl.ds(0, size)], out_sems.at[j]))
+            departures[-1].start()
+        upto = ready if i + 1 == chunks else ready - 1
+        for j in range(done, upto):
+            before = tiles_s[:, (j - 1) * LANES : j * LANES] if j else nothing
+            after = tiles_s[:, (j + 1) * LANES : (j + 2) * LANES] if j + 1 < strips else nothing
+            copies = jnp.dot(jnp.concatenate([before, after], axis=1), spread, preferred_element_type=F32)
+            copies_s[:, j * LANES : (j + 1) * LANES] = jnp.where(mask, copies, 0.0).astype(BF16)
+        done = upto
     edge = jnp.dot(same, copies_s[...], preferred_element_type=F32).astype(BF16)
     for j in range(strips):
-        out_ref[j, pl.ds(size, out_rows), :] = edge[:, j * LANES : (j + 1) * LANES]
+        edge_s[j] = edge[:, j * LANES : (j + 1) * LANES]
+    departures.append(pltpu.make_async_copy(edge_s, out_ref.at[:, pl.ds(size, out_rows)], edge_sem.at[0]))
+    departures[-1].start()
+    for departure in departures:
+        departure.wait()
 
 
 def pack(tiles, devices):
@@ -242,10 +276,16 @@
     return pl.pallas_call(
         functools.partial(pack_kernel, date_dev, row_count),
         out_shape=jax.ShapeDtypeStruct((devices, block_rows, LANES), BF16),
-        in_specs=[pl.BlockSpec(memory_space=pltpu.VMEM)],
-        out_specs=pl.BlockSpec(memory_space=pltpu.VMEM),
-        scratch_shapes=[pltpu.VMEM((size, col_total), BF16)],
-        compiler_params=pltpu.CompilerParams(vmem_limit_bytes=8 * size * col_total + 2**22),
+        in_specs=[pl.BlockSpec(memory_space=pl.ANY)],
+        out_specs=pl.BlockSpec(memory_space=pl.ANY),
+        scratch_shapes=[
+            pltpu.VMEM((size, col_total), BF16),
+            pltpu.VMEM((size, col_total), BF16),
+            pltpu.VMEM((devices, block_rows - size, LANES), BF16),
+            pltpu.SemaphoreType.DMA((4,)),
+            pltpu.SemaphoreType.DMA((devices,)),
+            pltpu.SemaphoreType.DMA((1,)),
+        ],
         name="pack",
     )(tiles.reshape(size, col_total))
 
@@ -259,14 +299,13 @@
     mean = jnp.sum(jnp.where(eye, sums[0:1], 0.0), axis=1, keepdims=True) / pixels
     slope = jnp.sum(jnp.where(eye, sums[1:2], 0.0), axis=1, keepdims=True) / square_sum
     trend = mean + slope * coord_ref[...]
-    rows = series_ref.shape[0] // dates
+    pad, rows = series_ref.shape[0] // dates, out_ref.shape[0] // dates
     chunks = sems.shape[0]
     per_chunk = dates // chunks
     copies = []
     for i in range(chunks):
         for d in range(i * per_chunk, (i + 1) * per_chunk):
-            at = pl.ds(d * rows, rows)
-            out_s[at, :] = series_ref[at, :] - trend[d : d + 1]
+            out_s[pl.ds(d * rows, rows), :] = series_ref[pl.ds(d * pad, rows), :] - trend[d : d + 1]
         at = pl.ds(i * per_chunk * rows, per_chunk * rows)
         copies.append(pltpu.make_async_copy(out_s.at[at], out_ref.at[at], sems.at[i]))
         copies[-1].start()
@@ -274,14 +313,14 @@
         copy.wait()
 
 
-def remove_trend(series, sums, more, coord, pixels, square_sum):
+def remove_trend(series, sums, more, coord, rows, pixels, square_sum):
     chunks = 8
     return pl.pallas_call(
         functools.partial(remove_kernel, pixels, square_sum),
-        out_shape=jax.ShapeDtypeStruct(series.shape, F32),
+        out_shape=jax.ShapeDtypeStruct((rows, LANES), F32),
         in_specs=[pl.BlockSpec(memory_space=pltpu.VMEM)] * 4,
         out_specs=pl.BlockSpec(memory_space=pl.ANY),
-        scratch_shapes=[pltpu.VMEM(series.shape, F32), pltpu.SemaphoreType.DMA((chunks,))],
+        scratch_shapes=[pltpu.VMEM((rows, LANES), F32), pltpu.SemaphoreType.DMA((chunks,))],
         compiler_params=pltpu.CompilerParams(vmem_limit_bytes=8 * series.size + 2**22),
         name="remove",
     )(series, sums, more, coord)
@@ -345,7 +384,8 @@
             for part in parts:
                 sums = sums + part
     square_sum = row_count * (col_total * col_total - 1) / (3 * col_total)
-    out = remove_trend(series, sums, jnp.stack(parts), columns[None], float(row_count * col_total), square_sum)
+    rows = date_total * row_count
+    out = remove_trend(series, sums, jnp.stack(parts), columns[None], rows, float(row_count * col_total), square_sum)
     return out.reshape(date_total, row_count, strip)
 
 

time: 56.1 us -> 55.5 us (0.989)
  local copies, waits for them, and re-layouts: 1.94 us -> 0.72 us
  Pallas kernels: 10 us -> 10.6 us
    pallas_call x1, Pallas kernels: 1.89 us -> 3.15 us  [pack(): pl.pallas_call(functools.partial(pack_kernel, date_dev, row_count), out_s...]
    unnamed x7 -> x5, local copies, waits for them, and re-layouts: 1.57 us -> 0.34 us
    pallas_call x1, Pallas kernels: 6.99 us -> 6.32 us  [observe_all(): pl.pallas_call(functools.partial(observe_kernel, row_count, unit_count),...]
where the time goes in v4:
time: 55.5 us; the launch traced here: 55.2 us
  starting transfers between devices  15.5 us (28%)
  waiting for transfers between devices  14.5 us (26%)
  other arithmetic  12.8 us (23%)
  Pallas kernels  10.6 us (19%)
  matrix products  0.81 us (1%)
  local copies, waits for them, and re-layouts  0.72 us (1%)
    all_to_all x1, waiting for transfers between devices, body(): blocks = lax.all_to_all(pack(slc_tiles, devices), 'gx', 0, 0, tiled=True)  9.43 us
    ppermute x6, starting transfers between devices, body(): lax.ppermute(sums, 'gx', [(s, s ^ k) for s in range(devices)])  7.95 us
    all_to_all x1, starting transfers between devices, body(): blocks = lax.all_to_all(pack(slc_tiles, devices), 'gx', 0, 0, tiled=True)  7.56 us
    another operation x3, other arithmetic, solve_matrix(): factor = jnp.linalg.cholesky(normal_matrix)  6.52 us
    pallas_call x1, Pallas kernels, observe_all(): pl.pallas_call(functools.partial(observe_kernel, row_count, unit_count),...  6.32 us
    another operation x2, other arithmetic, solve_matrix(): solved = jax.scipy.linalg.cho_solve((factor, True), columns)  5.55 us
    ppermute x6, waiting for transfers between devices, body(): lax.ppermute(sums, 'gx', [(s, s ^ k) for s in range(devices)])  5.11 us
    pallas_call x1, Pallas kernels, pack(): pl.pallas_call(functools.partial(pack_kernel, date_dev, row_count), out_s...  3.15 us
  transfers between devices with their start and end apart: 7, of which 5 were waited for; matrix products, arithmetic and copies ran while one was open for 26% of the time, Pallas kernels for 0%

profile of v4, /device:TPU:0, one launch (start us, length us, event | category | flops | bytes accessed | tf_op | source)
XLA Modules:
  0.0 55.2 jit_solution(5065238696625586937)
XLA Ops:
  0.0 3.1 %pack.1 = bf16[16,272,128]{2,1,0:T(8,128)(2,1)} custom-call(bf16[256,2048]{1,0:T(8,128)(2,1)} %bitcast.26), custom_call_target="tpu_custom_call" | custom-call | tf_op jit(solution)/shard_map/pack/pallas_call | solution.py:276
  3.2 7.6 %all-to-all-start = ((bf16[16,272,128]{2,1,0:T(8,128)(2,1)}), bf16[16,272,128]{2,1,0:T(8,128)(2,1)S(1)}, u32[]{:S(2)}, u32[]{:S(2)}) async-start(bf16[16,272,128]{2,1,0:T(8,128)(2,1)} %pack.1), calls=%async_computation | async-start | bytes 2228224 | tf_op jit(solution)/shard_map/all_to_all | solution.py:359
  11.1 5.8 %cholesky.17 = f32[64,64]{1,0:T(8,128)S(1)} custom-call(f32[64,64]{1,0:T(8,128)S(1)} %fusion.18), custom_call_target="Cholesky" | custom-call | tf_op jit(solution)/shard_map/jit(cholesky)/cholesky | solution.py:336
  17.0 0.6 %compare_reduce_fusion = pred[]{:T(512)} fusion(f32[64]{0:T(128)S(1)} %select_reduce_fusion), kind=kLoop, calls=%fused_computation.59 | loop fusion | flops 127 | bytes 257 | tf_op jit(solution)/shard_map/jit(cholesky)/cholesky | solution.py:336
  17.6 0.7 %fusion.9 = f32[1,64,64]{2,1,0:T(8,128)S(1)} fusion(f32[64,64]{1,0:T(8,128)S(1)} %cholesky.17, pred[]{:T(512)} %compare_reduce_fusion), kind=kLoop, calls=%fused_computation.30 | loop fusion | flops 16384 | bytes 32769 | tf_op jit(solution)/shard_map/jit(_cho_solve)/triangular_solve | solution.py:347
  18.3 0.3 copy.8
  18.6 0.2 fusion.12
  18.9 4.9 %custom-call.10 = f32[1,64,64]{1,2,0:T(8,128)S(1)} custom-call(f32[1,64,64]{2,1,0:T(8,128)S(1)} %fusion.9), custom_call_target="InvertDiagBlocksLowerTriangular" | custom-call | tf_op jit(solution)/shard_map/jit(_cho_solve)/triangular_solve | solution.py:347
  24.2 0.1 subtract_multiply_fusion
  24.3 0.3 fusion.15
  24.6 0.2 subtract_convert_fusion
  25.0 0.3 fusion.3.edge_ref
  25.3 9.4 %all-to-all-done.first_ref.next_ref = bf16[16,272,128]{2,1,0:T(8,128)(2,1)S(1)} async-done(((bf16[16,272,128]{2,1,0:T(8,128)(2,1)}), bf16[16,272,128]{2,1,0:T(8,128)(2,1)S(1)}, u32[]{:S(2)}, u32[]{:S(2)}) %all-to-all-start) | async-done | bytes 1114144 | tf_op jit(solution)/shard_map/all_to_all | solution.py:359
  34.7 6.3 %observe.1 = (f32[2560,128]{1,0:T(8,128)S(1)}, f32[2,64]{1,0:T(2,128)S(1)}) custom-call(bf16[16,272,128]{2,1,0:T(8,128)(2,1)S(1)} %all-to-all-done.first_ref.next_ref, bf16[16,272,128]{2,1,0:T(8,128)(2,1)S(1)} %all-to-all-done.first_ref.next_ref, f32[32,128]{1,0:T(8,128)S(1)} %constant_dynamic-slice_fusion.weight_ref, ...), custom_call_target="tpu_custom_call" | custom-call | tf_op jit(solution)/shard_map/observe/pallas_call | solution.py:198
  41.0 3.4 %collective-permute-start.2 = (f32[2,64]{1,0:T(2,128)S(1)}, f32[2,64]{1,0:T(2,128)S(1)}, u32[]{:S(2)}, u32[]{:S(2)}) collective-permute-start(f32[2,64]{1,0:T(2,128)S(1)} %get-tuple-element.8), channel_id=1, source_target_pairs={{0,12},{1,13},{2,14},{3,15},{4,8},{5,9},{6,10},{7,11},{8,4},{9,5},... | collective-permute-start | bytes 1544 | tf_op jit(solution)/shard_map/ppermute | solution.py:382
  44.5 2.1 %collective-permute-start.1 = (f32[2,64]{1,0:T(2,128)S(1)}, f32[2,64]{1,0:T(2,128)S(1)}, u32[]{:S(2)}, u32[]{:S(2)}) collective-permute-start(f32[2,64]{1,0:T(2,128)S(1)} %get-tuple-element.8), channel_id=1, source_target_pairs={{0,8},{1,9},{2,10},{3,11},{4,12},{5,13},{6,14},{7,15},{8,0},{9,1},... | collective-permute-start | bytes 1544 | tf_op jit(solution)/shard_map/ppermute | solution.py:382
  46.6 0.5 collective-permute-start
  47.1 1.8 %collective-permute-done.1 = f32[2,64]{1,0:T(2,128)S(1)} collective-permute-done((f32[2,64]{1,0:T(2,128)S(1)}, f32[2,64]{1,0:T(2,128)S(1)}, u32[]{:S(2)}, u32[]{:S(2)}) %collective-permute-start.1) | collective-permute-done | bytes 544 | tf_op jit(solution)/shard_map/ppermute | solution.py:382
  48.9 1.2 %collective-permute-done = f32[2,64]{1,0:T(2,128)S(1)} collective-permute-done((f32[2,64]{1,0:T(2,128)S(1)}, f32[2,64]{1,0:T(2,128)S(1)}, u32[]{:S(2)}, u32[]{:S(2)}) %collective-permute-start) | collective-permute-done | bytes 544 | tf_op jit(solution)/shard_map/ppermute | solution.py:382
  50.2 0.3 collective-permute-start.5
  50.5 1.5 %collective-permute-start.4 = (f32[2,64]{1,0:T(2,128)S(1)}, f32[2,64]{1,0:T(2,128)S(1)}, u32[]{:S(2)}, u32[]{:S(2)}) collective-permute-start(f32[2,64]{1,0:T(2,128)S(1)} %add_add_fusion.sums_ref), channel_id=1, source_target_pairs={{0,2},{1,3},{2,0},{3,1},{4,6},{5,7},{6,4},{7,5},{8,10},{9,11},{10,... | collective-permute-start | bytes 1544 | tf_op jit(solution)/shard_map/ppermute | solution.py:382
  52.1 1.1 %collective-permute-done.5 = f32[2,64]{1,0:T(2,128)S(1)} collective-permute-done((f32[2,64]{1,0:T(2,128)S(1)}, f32[2,64]{1,0:T(2,128)S(1)}, u32[]{:S(2)}, u32[]{:S(2)}) %collective-permute-start.5) | collective-permute-done | bytes 544 | tf_op jit(solution)/shard_map/ppermute | solution.py:382
  53.2 0.9 %collective-permute-done.4 = f32[2,64]{1,0:T(2,128)S(1)} collective-permute-done((f32[2,64]{1,0:T(2,128)S(1)}, f32[2,64]{1,0:T(2,128)S(1)}, u32[]{:S(2)}, u32[]{:S(2)}) %collective-permute-start.4) | collective-permute-done | bytes 544 | tf_op jit(solution)/shard_map/ppermute | solution.py:382
  54.1 1.1 %remove.1 = f32[2048,128]{1,0:T(8,128)} custom-call(f32[2560,128]{1,0:T(8,128)S(1)} %get-tuple-element.7.series_ref, f32[2,64]{1,0:T(2,128)S(1)} %add_add_fusion.sums_ref, f32[3,2,64]{2,1,0:T(2,128)S(1)} %pad_maximum_fusion.2.more_ref, f32[1,128]{1,0:T(1,128)S(1)} %multiply_add_fusion.1.coord_ref), custom_call_target="tpu_custom_call" | custom-call | tf_op jit(solution)/shard_map/remove/pallas_call | solution.py:318
  (33 shorter events, 0.9 us)
Async XLA Ops:
  3.2 7.6 %copy-start.1 = (s32[192,2]{0,1:T(2,128)S(1)}, s32[192,2]{0,1:T(2,128)}, u32[]{:S(2)}) copy-start(s32[192,2]{0,1:T(2,128)} %param.5) | copy-start | bytes 4612
  3.2 15.1 %copy-start = (f32[32,2048]{1,0:T(8,128)S(1)}, f32[32,2048]{1,0:T(8,128)}, u32[]{:S(2)}) copy-start(f32[32,2048]{1,0:T(8,128)} %param.4) | copy-start | bytes 786436
  3.2 31.5 %all-to-all-start = ((bf16[16,272,128]{2,1,0:T(8,128)(2,1)}), bf16[16,272,128]{2,1,0:T(8,128)(2,1)S(1)}, u32[]{:S(2)}, u32[]{:S(2)}) async-start(bf16[16,272,128]{2,1,0:T(8,128)(2,1)} %pack.1), calls=%async_computation | async-start | bytes 2228224 | tf_op jit(solution)/shard_map/all_to_all | solution.py:359
  41.0 6.1 %collective-permute-start.2 = (f32[2,64]{1,0:T(2,128)S(1)}, f32[2,64]{1,0:T(2,128)S(1)}, u32[]{:S(2)}, u32[]{:S(2)}) collective-permute-start(f32[2,64]{1,0:T(2,128)S(1)} %get-tuple-element.8), channel_id=1, source_target_pairs={{0,12},{1,13},{2,14},{3,15},{4,8},{5,9},{6,10},{7,11},{8,4},{9,5},... | collective-permute-start | bytes 1544 | tf_op jit(solution)/shard_map/ppermute | solution.py:382
  44.5 4.5 %collective-permute-start.1 = (f32[2,64]{1,0:T(2,128)S(1)}, f32[2,64]{1,0:T(2,128)S(1)}, u32[]{:S(2)}, u32[]{:S(2)}) collective-permute-start(f32[2,64]{1,0:T(2,128)S(1)} %get-tuple-element.8), channel_id=1, source_target_pairs={{0,8},{1,9},{2,10},{3,11},{4,12},{5,13},{6,14},{7,15},{8,0},{9,1},... | collective-permute-start | bytes 1544 | tf_op jit(solution)/shard_map/ppermute | solution.py:382
  46.6 3.6 %collective-permute-start = (f32[2,64]{1,0:T(2,128)S(1)}, f32[2,64]{1,0:T(2,128)S(1)}, u32[]{:S(2)}, u32[]{:S(2)}) collective-permute-start(f32[2,64]{1,0:T(2,128)S(1)} %get-tuple-element.8), channel_id=1, source_target_pairs={{0,4},{1,5},{2,6},{3,7},{4,0},{5,1},{6,2},{7,3},{8,12},{9,13},{10,... | collective-permute-start | bytes 1544 | tf_op jit(solution)/shard_map/ppermute | solution.py:382
  50.2 3.0 %collective-permute-start.5 = (f32[2,64]{1,0:T(2,128)S(1)}, f32[2,64]{1,0:T(2,128)S(1)}, u32[]{:S(2)}, u32[]{:S(2)}) collective-permute-start(f32[2,64]{1,0:T(2,128)S(1)} %add_add_fusion.sums_ref), channel_id=1, source_target_pairs={{0,3},{1,2},{2,1},{3,0},{4,7},{5,6},{6,5},{7,4},{8,11},{9,10},{10,... | collective-permute-start | bytes 1544 | tf_op jit(solution)/shard_map/ppermute | solution.py:382
  50.5 3.6 %collective-permute-start.4 = (f32[2,64]{1,0:T(2,128)S(1)}, f32[2,64]{1,0:T(2,128)S(1)}, u32[]{:S(2)}, u32[]{:S(2)}) collective-permute-start(f32[2,64]{1,0:T(2,128)S(1)} %add_add_fusion.sums_ref), channel_id=1, source_target_pairs={{0,2},{1,3},{2,0},{3,1},{4,6},{5,7},{6,4},{7,5},{8,10},{9,11},{10,... | collective-permute-start | bytes 1544 | tf_op jit(solution)/shard_map/ppermute | solution.py:382
  52.0 2.1 %collective-permute-start.3 = (f32[2,64]{1,0:T(2,128)S(1)}, f32[2,64]{1,0:T(2,128)S(1)}, u32[]{:S(2)}, u32[]{:S(2)}) collective-permute-start(f32[2,64]{1,0:T(2,128)S(1)} %add_add_fusion.sums_ref), channel_id=1, source_target_pairs={{0,1},{1,0},{2,3},{3,2},{4,5},{5,4},{6,7},{7,6},{8,9},{9,8},{10,11... | collective-permute-start | bytes 1544 | tf_op jit(solution)/shard_map/ppermute | solution.py:382

commit v5 on v4

--- a/solution.py
+++ b/solution.py
@@ -60,28 +60,29 @@
 
 def observe_kernel(
     row_count, unit_count,
-    first_ref, next_ref, weight_ref, edge_weight_ref, band_ref, edge_ref, solve_ref, coord_ref,
+    blocks_ref, weight_ref, edge_weight_ref, band_ref, edge_ref, solve_ref, coord_ref,
     series_ref, sums_ref,
     re_s, im_s, wre_s, wim_s, pw_s, hre_s, him_s, hwre_s, hwim_s, obs_s,
 ):
-    unit = pl.program_id(0)
-    slots = (unit_count + 1) * SUB
+    slots = (unit_count + 3) * SUB
     halves = row_count // HALF
-    per_unit, block_rows, _ = next_ref.shape
+    sources = blocks_ref.shape[0]
+    per_unit = sources // unit_count
     date_dev = SUB // per_unit
     hbase = 2 * date_dev * row_count
     pad = series_ref.shape[0] // solve_ref.shape[0] * 2
 
-    def place(group_ref, new):
+    def place(group, new):
         for s in range(per_unit):
+            source = group * per_unit + s
             for d in range(date_dev):
                 for c, dst in ((0, re_s), (1, im_s)):
                     start = (d * 2 + c) * row_count
-                    values = group_ref[s, pl.ds(start, row_count), :].astype(F32)
+                    values = blocks_ref[source, pl.ds(start, row_count), :].astype(F32)
                     for g in range(row_count // SUB):
                         at = pl.ds(g * SUB * slots + new + s * date_dev + d, SUB, stride=slots)
                         dst[at, :] = values[g * SUB : (g + 1) * SUB]
-            edge = group_ref[s, pl.ds(hbase, 2 * halves * date_dev), :].astype(F32)
+            edge = blocks_ref[source, pl.ds(hbase, 2 * halves * date_dev), :].astype(F32)
             for c, dst in ((0, hre_s), (1, him_s)):
                 for h in range(halves):
                     start = (c * halves + h) * date_dev
@@ -124,8 +125,8 @@
             out.append(summed[r * SUB : (r + 1) * SUB] + jnp.where(at_edge, rolled, 0.0))
         return out
 
-    def bring(group_ref, new):
-        place(group_ref, new)
+    def bring(group, new):
+        place(lax.rem(group, unit_count), new)
         edges = at_edges([power(hre_s, him_s, hwre_s, hwim_s, edge_weight_ref, halves, new)])
         image = power(re_s, im_s, wre_s, wim_s, weight_ref, row_count, new)
         for r, value in enumerate(look(image, edges)):
@@ -133,51 +134,54 @@
 
     combos = unit_count * SUB * LAGS
 
-    @pl.when(unit == 0)
-    def _():
-        bring(first_ref, pl.multiple_of(unit * SUB, SUB))
-
-    old = pl.multiple_of(unit * SUB, SUB)
-    @pl.when(unit < unit_count)
-    def _():
-        bring(next_ref, pl.multiple_of(old + SUB, SUB))
-
-    edges = at_edges([cross(hre_s, him_s, hwre_s, hwim_s, halves, lag, old) for lag in range(1, LAGS + 1)])
-
-    def observed(lag):
-        image = cross(re_s, im_s, wre_s, wim_s, row_count, lag, old)
-        out = []
-        for r, value in enumerate(look(image, edges[(lag - 1) * SUB : lag * SUB])):
-            p = pw_s[pl.ds(r * slots + old, SUB), :]
-            q = pw_s[pl.ds(r * slots + old + lag, SUB), :]
-            out.append(value * lax.rsqrt(p * q + 1e-06))
-        return out
-
-    for lag in range(1, LAGS + 1, 2):
-        first, second = observed(lag), observed(lag + 1)
-        for r in range(row_count):
-            at = pl.multiple_of(r * combos + unit * (SUB * LAGS) + (lag - 1) * SUB, 2 * SUB)
-            obs_s[pl.ds(at, 2 * SUB), :] = jnp.concatenate([first[r], second[r]], axis=0).astype(BF16)
-
-    @pl.when(unit == unit_count - 1)
-    def _():
-        solve = solve_ref[...]
-        date_total = solve.shape[0] // 2
-        mean = jnp.zeros((date_total, LANES), F32)
-        for r in range(0, row_count, 2):
-            pair = [obs_s[pl.ds((r + i) * combos, combos), :] for i in range(2)]
-            both = jnp.dot(solve, jnp.concatenate(pair, axis=1), preferred_element_type=F32)
-            both = both[:date_total] + both[date_total:]
-            for i in range(2):
-                series = both[:, i * LANES : (i + 1) * LANES]
-                for g in range(date_total // SUB):
-                    at = pl.ds(g * SUB * pad + r + i, SUB, stride=pad)
-                    series_ref[at, :] = series[g * SUB : (g + 1) * SUB]
-                mean = mean + series
-        eye = iota2((date_total, date_total), 0) == iota2((date_total, date_total), 1)
-        for i, part in enumerate((mean, mean * coord_ref[...])):
-            column = jnp.sum(part, axis=1, keepdims=True)
-            sums_ref[pl.ds(i, 1), :] = jnp.sum(jnp.where(eye, column, 0.0), axis=0, keepdims=True)
+    together = 3 if (unit_count + 1) % 3 == 0 else 2
+
+    def bring_some(step, carry):
+        for g in range(together):
+            bring(together * step + g, pl.multiple_of((together * step + g) * SUB, SUB))
+        return carry
+
+    lax.fori_loop(0, -(-(unit_count + 1) // together), bring_some, 0)
+
+    def observe_unit(unit, carry):
+        old = pl.multiple_of(unit * SUB, SUB)
+        edges = at_edges([cross(hre_s, him_s, hwre_s, hwim_s, halves, lag, old) for lag in range(1, LAGS + 1)])
+
+        def observed(lag):
+            image = cross(re_s, im_s, wre_s, wim_s, row_count, lag, old)
+            out = []
+            for r, value in enumerate(look(image, edges[(lag - 1) * SUB : lag * SUB])):
+                p = pw_s[pl.ds(r * slots + old, SUB), :]
+                q = pw_s[pl.ds(r * slots + old + lag, SUB), :]
+                out.append(value * lax.rsqrt(p * q + 1e-06))
+            return out
+
+        for lag in range(1, LAGS + 1, 2):
+            first, second = observed(lag), observed(lag + 1)
+            for r in range(row_count):
+                at = pl.multiple_of(r * combos + unit * (SUB * LAGS) + (lag - 1) * SUB, 2 * SUB)
+                obs_s[pl.ds(at, 2 * SUB), :] = jnp.concatenate([first[r], second[r]], axis=0).astype(BF16)
+        return carry
+
+    lax.fori_loop(0, unit_count, observe_unit, 0)
+
+    solve = solve_ref[...]
+    date_total = solve.shape[0] // 2
+    mean = jnp.zeros((date_total, LANES), F32)
+    for r in range(0, row_count, 2):
+        pair = [obs_s[pl.ds((r + i) * combos, combos), :] for i in range(2)]
+        both = jnp.dot(solve, jnp.concatenate(pair, axis=1), preferred_element_type=F32)
+        both = both[:date_total] + both[date_total:]
+        for i in range(2):
+            series = both[:, i * LANES : (i + 1) * LANES]
+            for g in range(date_total // SUB):
+                at = pl.ds(g * SUB * pad + r + i, SUB, stride=pad)
+                series_ref[at, :] = series[g * SUB : (g + 1) * SUB]
+            mean = mean + series
+    eye = iota2((date_total, date_total), 0) == iota2((date_total, date_total), 1)
+    for i, part in enumerate((mean, mean * coord_ref[...])):
+        column = jnp.sum(part, axis=1, keepdims=True)
+        sums_ref[pl.ds(i, 1), :] = jnp.sum(jnp.where(eye, column, 0.0), axis=0, keepdims=True)
 
 
 def observe_all(blocks, weight, edge_weight, solve, coord, row_count, date_dev):
@@ -187,9 +191,8 @@
     date_total = unit_count * SUB
     combos = date_total * LAGS
     halves = row_count // HALF
-    slots = (unit_count + 1) * SUB
+    slots = (unit_count + 3) * SUB
     pad = row_count + SUB
-    whole = lambda a: pl.BlockSpec(a.shape, lambda u: (0,) * a.ndim)
     band, edge = column_band(), edge_matrix(row_count)
     scratch = [pltpu.VMEM((row_count * slots, LANES), F32)] * 5
     scratch += [pltpu.VMEM((halves * slots, LANES), F32)] * 4
@@ -197,26 +200,16 @@
     words = row_count * LANES * (5 * slots + combos // 2 + 3 * date_total) + date_total * LANES * combos // 64
     return pl.pallas_call(
         functools.partial(observe_kernel, row_count, unit_count),
-        grid=(unit_count,),
         out_shape=(
             jax.ShapeDtypeStruct((date_total * pad, LANES), F32),
             jax.ShapeDtypeStruct((2, date_total), F32),
         ),
-        in_specs=[
-            pl.BlockSpec((per_unit, block_rows, LANES), lambda u: (0, 0, 0)),
-            pl.BlockSpec((per_unit, block_rows, LANES), lambda u: (lax.rem(u + 1, unit_count), 0, 0)),
-            whole(weight), whole(edge_weight), whole(band), whole(edge), whole(solve), whole(coord),
-        ],
-        out_specs=(
-            pl.BlockSpec((date_total * pad, LANES), lambda u: (0, 0)),
-            pl.BlockSpec((2, date_total), lambda u: (0, 0)),
-        ),
+        in_specs=[pl.BlockSpec(memory_space=pltpu.VMEM)] * 7,
+        out_specs=[pl.BlockSpec(memory_space=pltpu.VMEM)] * 2,
         scratch_shapes=scratch,
-        compiler_params=pltpu.CompilerParams(
-            dimension_semantics=("arbitrary",), vmem_limit_bytes=min(4 * words + 2**23, 2**26 - 2**17)
-        ),
+        compiler_params=pltpu.CompilerParams(vmem_limit_bytes=min(4 * words + 2**23, 2**26 - 2**17)),
         name="observe",
-    )(blocks, blocks, weight, edge_weight, band, edge, solve, coord)
+    )(blocks, weight, edge_weight, band, edge, solve, coord)
 
 
 def pack_kernel(date_dev, row_count, tiles_ref, out_ref, tiles_s, copies_s, edge_s, in_sems, out_sems, edge_sem):

time: 55.5 us -> 54.3 us (0.978)
  Pallas kernels: 10.6 us -> 9.44 us
    pallas_call x1, Pallas kernels: 6.32 us -> 5.17 us  [observe_all(): pl.pallas_call(functools.partial(observe_kernel, row_count, unit_count),...]
  transfers between devices with their start and end apart: 7 -> 7, of which waited for: 5 -> 5; matrix products, arithmetic and copies ran while one was open for 26% -> 27% of each run, Pallas kernels for 0% -> 0%
where the time goes in v5:
time: 54.3 us; the launch traced here: 54.1 us
  starting transfers between devices  15.5 us (29%)
  waiting for transfers between devices  14.5 us (27%)
  other arithmetic  12.8 us (24%)
  Pallas kernels  9.44 us (17%)
  matrix products  0.81 us (1%)
  local copies, waits for them, and re-layouts  0.72 us (1%)
    all_to_all x1, waiting for transfers between devices, body(): blocks = lax.all_to_all(pack(slc_tiles, devices), 'gx', 0, 0, tiled=True)  9.43 us
    ppermute x6, starting transfers between devices, body(): lax.ppermute(sums, 'gx', [(s, s ^ k) for s in range(devices)])  7.95 us
    all_to_all x1, starting transfers between devices, body(): blocks = lax.all_to_all(pack(slc_tiles, devices), 'gx', 0, 0, tiled=True)  7.56 us
    another operation x3, other arithmetic, solve_matrix(): factor = jnp.linalg.cholesky(normal_matrix)  6.52 us
    another operation x2, other arithmetic, solve_matrix(): solved = jax.scipy.linalg.cho_solve((factor, True), columns)  5.55 us
    pallas_call x1, Pallas kernels, observe_all(): pl.pallas_call(functools.partial(observe_kernel, row_count, unit_count),...  5.17 us
    ppermute x6, waiting for transfers between devices, body(): lax.ppermute(sums, 'gx', [(s, s ^ k) for s in range(devices)])  5.11 us
    pallas_call x1, Pallas kernels, pack(): pl.pallas_call(functools.partial(pack_kernel, date_dev, row_count), out_s...  3.15 us
  transfers between devices with their start and end apart: 7, of which 5 were waited for; matrix products, arithmetic and copies ran while one was open for 27% of the time, Pallas kernels for 0%

profile of v5, /device:TPU:0, one launch (start us, length us, event | category | flops | bytes accessed | tf_op | source)
XLA Modules:
  0.0 54.1 jit_solution(8628660777325734611)
XLA Ops:
  0.0 3.1 %pack.1 = bf16[16,272,128]{2,1,0:T(8,128)(2,1)} custom-call(bf16[256,2048]{1,0:T(8,128)(2,1)} %bitcast.26), custom_call_target="tpu_custom_call" | custom-call | tf_op jit(solution)/shard_map/pack/pallas_call | solution.py:269
  3.2 7.6 %all-to-all-start = ((bf16[16,272,128]{2,1,0:T(8,128)(2,1)}), bf16[16,272,128]{2,1,0:T(8,128)(2,1)S(1)}, u32[]{:S(2)}, u32[]{:S(2)}) async-start(bf16[16,272,128]{2,1,0:T(8,128)(2,1)} %pack.1), calls=%async_computation | async-start | bytes 2228224 | tf_op jit(solution)/shard_map/all_to_all | solution.py:352
  11.1 5.8 %cholesky.17 = f32[64,64]{1,0:T(8,128)S(1)} custom-call(f32[64,64]{1,0:T(8,128)S(1)} %fusion.18), custom_call_target="Cholesky" | custom-call | tf_op jit(solution)/shard_map/jit(cholesky)/cholesky | solution.py:329
  17.0 0.6 %compare_reduce_fusion = pred[]{:T(512)} fusion(f32[64]{0:T(128)S(1)} %select_reduce_fusion), kind=kLoop, calls=%fused_computation.59 | loop fusion | flops 127 | bytes 257 | tf_op jit(solution)/shard_map/jit(cholesky)/cholesky | solution.py:329
  17.6 0.7 %fusion.9 = f32[1,64,64]{2,1,0:T(8,128)S(1)} fusion(f32[64,64]{1,0:T(8,128)S(1)} %cholesky.17, pred[]{:T(512)} %compare_reduce_fusion), kind=kLoop, calls=%fused_computation.30 | loop fusion | flops 16384 | bytes 32769 | tf_op jit(solution)/shard_map/jit(_cho_solve)/triangular_solve | solution.py:340
  18.3 0.3 copy.8
  18.6 0.2 fusion.12
  18.9 4.9 %custom-call.10 = f32[1,64,64]{1,2,0:T(8,128)S(1)} custom-call(f32[1,64,64]{2,1,0:T(8,128)S(1)} %fusion.9), custom_call_target="InvertDiagBlocksLowerTriangular" | custom-call | tf_op jit(solution)/shard_map/jit(_cho_solve)/triangular_solve | solution.py:340
  24.2 0.1 subtract_multiply_fusion
  24.3 0.3 fusion.15
  24.6 0.2 subtract_convert_fusion
  25.0 0.3 fusion.3.edge_ref
  25.3 9.4 %all-to-all-done.blocks_ref = bf16[16,272,128]{2,1,0:T(8,128)(2,1)S(1)} async-done(((bf16[16,272,128]{2,1,0:T(8,128)(2,1)}), bf16[16,272,128]{2,1,0:T(8,128)(2,1)S(1)}, u32[]{:S(2)}, u32[]{:S(2)}) %all-to-all-start) | async-done | bytes 1114144 | tf_op jit(solution)/shard_map/all_to_all | solution.py:352
  34.7 5.2 %observe.1 = (f32[2560,128]{1,0:T(8,128)S(1)}, f32[2,64]{1,0:T(2,128)S(1)}) custom-call(bf16[16,272,128]{2,1,0:T(8,128)(2,1)S(1)} %all-to-all-done.blocks_ref, f32[32,128]{1,0:T(8,128)S(1)} %constant_dynamic-slice_fusion.weight_ref, f32[2,128]{1,0:T(2,128)S(1)} %reshape.150.edge_weight_ref, bf16[256,128]{1,0:T(8,128)(2,1)S(1)} %fusion.7.band_ref, ...), custom_call_target="tpu_custom_call" | custom-call | tf_op jit(solution)/shard_map/observe/pallas_call | solution.py:201
  39.9 3.4 %collective-permute-start.2 = (f32[2,64]{1,0:T(2,128)S(1)}, f32[2,64]{1,0:T(2,128)S(1)}, u32[]{:S(2)}, u32[]{:S(2)}) collective-permute-start(f32[2,64]{1,0:T(2,128)S(1)} %get-tuple-element.8), channel_id=1, source_target_pairs={{0,12},{1,13},{2,14},{3,15},{4,8},{5,9},{6,10},{7,11},{8,4},{9,5},... | collective-permute-start | bytes 1544 | tf_op jit(solution)/shard_map/ppermute | solution.py:375
  43.3 2.1 %collective-permute-start.1 = (f32[2,64]{1,0:T(2,128)S(1)}, f32[2,64]{1,0:T(2,128)S(1)}, u32[]{:S(2)}, u32[]{:S(2)}) collective-permute-start(f32[2,64]{1,0:T(2,128)S(1)} %get-tuple-element.8), channel_id=1, source_target_pairs={{0,8},{1,9},{2,10},{3,11},{4,12},{5,13},{6,14},{7,15},{8,0},{9,1},... | collective-permute-start | bytes 1544 | tf_op jit(solution)/shard_map/ppermute | solution.py:375
  45.4 0.5 collective-permute-start
  45.9 1.8 %collective-permute-done.1 = f32[2,64]{1,0:T(2,128)S(1)} collective-permute-done((f32[2,64]{1,0:T(2,128)S(1)}, f32[2,64]{1,0:T(2,128)S(1)}, u32[]{:S(2)}, u32[]{:S(2)}) %collective-permute-start.1) | collective-permute-done | bytes 544 | tf_op jit(solution)/shard_map/ppermute | solution.py:375
  47.8 1.2 %collective-permute-done = f32[2,64]{1,0:T(2,128)S(1)} collective-permute-done((f32[2,64]{1,0:T(2,128)S(1)}, f32[2,64]{1,0:T(2,128)S(1)}, u32[]{:S(2)}, u32[]{:S(2)}) %collective-permute-start) | collective-permute-done | bytes 544 | tf_op jit(solution)/shard_map/ppermute | solution.py:375
  49.0 0.3 collective-permute-start.5
  49.4 1.5 %collective-permute-start.4 = (f32[2,64]{1,0:T(2,128)S(1)}, f32[2,64]{1,0:T(2,128)S(1)}, u32[]{:S(2)}, u32[]{:S(2)}) collective-permute-start(f32[2,64]{1,0:T(2,128)S(1)} %add_add_fusion.sums_ref), channel_id=1, source_target_pairs={{0,2},{1,3},{2,0},{3,1},{4,6},{5,7},{6,4},{7,5},{8,10},{9,11},{10,... | collective-permute-start | bytes 1544 | tf_op jit(solution)/shard_map/ppermute | solution.py:375
  50.9 1.1 %collective-permute-done.5 = f32[2,64]{1,0:T(2,128)S(1)} collective-permute-done((f32[2,64]{1,0:T(2,128)S(1)}, f32[2,64]{1,0:T(2,128)S(1)}, u32[]{:S(2)}, u32[]{:S(2)}) %collective-permute-start.5) | collective-permute-done | bytes 544 | tf_op jit(solution)/shard_map/ppermute | solution.py:375
  52.0 0.9 %collective-permute-done.4 = f32[2,64]{1,0:T(2,128)S(1)} collective-permute-done((f32[2,64]{1,0:T(2,128)S(1)}, f32[2,64]{1,0:T(2,128)S(1)}, u32[]{:S(2)}, u32[]{:S(2)}) %collective-permute-start.4) | collective-permute-done | bytes 544 | tf_op jit(solution)/shard_map/ppermute | solution.py:375
  52.9 1.1 %remove.1 = f32[2048,128]{1,0:T(8,128)} custom-call(f32[2560,128]{1,0:T(8,128)S(1)} %get-tuple-element.7.series_ref, f32[2,64]{1,0:T(2,128)S(1)} %add_add_fusion.sums_ref, f32[3,2,64]{2,1,0:T(2,128)S(1)} %pad_maximum_fusion.2.more_ref, f32[1,128]{1,0:T(1,128)S(1)} %multiply_add_fusion.1.coord_ref), custom_call_target="tpu_custom_call" | custom-call | tf_op jit(solution)/shard_map/remove/pallas_call | solution.py:311
  (33 shorter events, 0.9 us)
Async XLA Ops:
  3.2 7.6 %copy-start.1 = (s32[192,2]{0,1:T(2,128)S(1)}, s32[192,2]{0,1:T(2,128)}, u32[]{:S(2)}) copy-start(s32[192,2]{0,1:T(2,128)} %param.5) | copy-start | bytes 4612
  3.2 15.1 %copy-start = (f32[32,2048]{1,0:T(8,128)S(1)}, f32[32,2048]{1,0:T(8,128)}, u32[]{:S(2)}) copy-start(f32[32,2048]{1,0:T(8,128)} %param.4) | copy-start | bytes 786436
  3.2 31.5 %all-to-all-start = ((bf16[16,272,128]{2,1,0:T(8,128)(2,1)}), bf16[16,272,128]{2,1,0:T(8,128)(2,1)S(1)}, u32[]{:S(2)}, u32[]{:S(2)}) async-start(bf16[16,272,128]{2,1,0:T(8,128)(2,1)} %pack.1), calls=%async_computation | async-start | bytes 2228224 | tf_op jit(solution)/shard_map/all_to_all | solution.py:352
  39.9 6.1 %collective-permute-start.2 = (f32[2,64]{1,0:T(2,128)S(1)}, f32[2,64]{1,0:T(2,128)S(1)}, u32[]{:S(2)}, u32[]{:S(2)}) collective-permute-start(f32[2,64]{1,0:T(2,128)S(1)} %get-tuple-element.8), channel_id=1, source_target_pairs={{0,12},{1,13},{2,14},{3,15},{4,8},{5,9},{6,10},{7,11},{8,4},{9,5},... | collective-permute-start | bytes 1544 | tf_op jit(solution)/shard_map/ppermute | solution.py:375
  43.3 4.5 %collective-permute-start.1 = (f32[2,64]{1,0:T(2,128)S(1)}, f32[2,64]{1,0:T(2,128)S(1)}, u32[]{:S(2)}, u32[]{:S(2)}) collective-permute-start(f32[2,64]{1,0:T(2,128)S(1)} %get-tuple-element.8), channel_id=1, source_target_pairs={{0,8},{1,9},{2,10},{3,11},{4,12},{5,13},{6,14},{7,15},{8,0},{9,1},... | collective-permute-start | bytes 1544 | tf_op jit(solution)/shard_map/ppermute | solution.py:375
  45.4 3.6 %collective-permute-start = (f32[2,64]{1,0:T(2,128)S(1)}, f32[2,64]{1,0:T(2,128)S(1)}, u32[]{:S(2)}, u32[]{:S(2)}) collective-permute-start(f32[2,64]{1,0:T(2,128)S(1)} %get-tuple-element.8), channel_id=1, source_target_pairs={{0,4},{1,5},{2,6},{3,7},{4,0},{5,1},{6,2},{7,3},{8,12},{9,13},{10,... | collective-permute-start | bytes 1544 | tf_op jit(solution)/shard_map/ppermute | solution.py:375
  49.0 3.0 %collective-permute-start.5 = (f32[2,64]{1,0:T(2,128)S(1)}, f32[2,64]{1,0:T(2,128)S(1)}, u32[]{:S(2)}, u32[]{:S(2)}) collective-permute-start(f32[2,64]{1,0:T(2,128)S(1)} %add_add_fusion.sums_ref), channel_id=1, source_target_pairs={{0,3},{1,2},{2,1},{3,0},{4,7},{5,6},{6,5},{7,4},{8,11},{9,10},{10,... | collective-permute-start | bytes 1544 | tf_op jit(solution)/shard_map/ppermute | solution.py:375
  49.4 3.6 %collective-permute-start.4 = (f32[2,64]{1,0:T(2,128)S(1)}, f32[2,64]{1,0:T(2,128)S(1)}, u32[]{:S(2)}, u32[]{:S(2)}) collective-permute-start(f32[2,64]{1,0:T(2,128)S(1)} %add_add_fusion.sums_ref), channel_id=1, source_target_pairs={{0,2},{1,3},{2,0},{3,1},{4,6},{5,7},{6,4},{7,5},{8,10},{9,11},{10,... | collective-permute-start | bytes 1544 | tf_op jit(solution)/shard_map/ppermute | solution.py:375
  50.9 2.1 %collective-permute-start.3 = (f32[2,64]{1,0:T(2,128)S(1)}, f32[2,64]{1,0:T(2,128)S(1)}, u32[]{:S(2)}, u32[]{:S(2)}) collective-permute-start(f32[2,64]{1,0:T(2,128)S(1)} %add_add_fusion.sums_ref), channel_id=1, source_target_pairs={{0,1},{1,0},{2,3},{3,2},{4,5},{5,4},{6,7},{7,6},{8,9},{9,8},{10,11... | collective-permute-start | bytes 1544 | tf_op jit(solution)/shard_map/ppermute | solution.py:375

commit v6 on v5

--- a/solution.py
+++ b/solution.py
@@ -217,11 +217,10 @@
     size, col_total = tiles_s.shape
     halves = row_count // HALF
     chunks = in_sems.shape[0]
-    per_chunk = strips // chunks
     arrivals = []
     for i in range(chunks):
-        at = pl.ds(i * per_chunk * LANES, per_chunk * LANES)
-        arrivals.append(pltpu.make_async_copy(tiles_ref.at[:, at], tiles_s.at[:, at], in_sems.at[i]))
+        at = pl.ds(i * (size // chunks), size // chunks)
+        arrivals.append(pltpu.make_async_copy(tiles_ref.at[at], tiles_s.at[at], in_sems.at[i]))
         arrivals[-1].start()
     source, lane = iota2((2 * LANES, LANES), 0), iota2((2 * LANES, LANES), 1) % EDGE
     spread = (lane == jnp.where(source < LANES, source - (LANES - RIM), source - LANES + RIM)) & (
@@ -237,22 +236,18 @@
         & (target // date_dev % halves == row // HALF % halves)
     ).astype(BF16)
     nothing = jnp.zeros((size, LANES), BF16)
+    for arrival in arrivals:
+        arrival.wait()
     departures = []
-    done = 0
-    for i in range(chunks):
-        arrivals[i].wait()
-        ready = (i + 1) * per_chunk
-        for j in range(ready - per_chunk, ready):
-            strip = tiles_s.at[:, pl.ds(j * LANES, LANES)]
-            departures.append(pltpu.make_async_copy(strip, out_ref.at[j, pl.ds(0, size)], out_sems.at[j]))
-            departures[-1].start()
-        upto = ready if i + 1 == chunks else ready - 1
-        for j in range(done, upto):
-            before = tiles_s[:, (j - 1) * LANES : j * LANES] if j else nothing
-            after = tiles_s[:, (j + 1) * LANES : (j + 2) * LANES] if j + 1 < strips else nothing
-            copies = jnp.dot(jnp.concatenate([before, after], axis=1), spread, preferred_element_type=F32)
-            copies_s[:, j * LANES : (j + 1) * LANES] = jnp.where(mask, copies, 0.0).astype(BF16)
-        done = upto
+    for j in range(strips):
+        strip = tiles_s.at[:, pl.ds(j * LANES, LANES)]
+        departures.append(pltpu.make_async_copy(strip, out_ref.at[j, pl.ds(0, size)], out_sems.at[j]))
+        departures[-1].start()
+    for j in range(strips):
+        before = tiles_s[:, (j - 1) * LANES : j * LANES] if j else nothing
+        after = tiles_s[:, (j + 1) * LANES : (j + 2) * LANES] if j + 1 < strips else nothing
+        copies = jnp.dot(jnp.concatenate([before, after], axis=1), spread, preferred_element_type=F32)
+        copies_s[:, j * LANES : (j + 1) * LANES] = jnp.where(mask, copies, 0.0).astype(BF16)
     edge = jnp.dot(same, copies_s[...], preferred_element_type=F32).astype(BF16)
     for j in range(strips):
         edge_s[j] = edge[:, j * LANES : (j + 1) * LANES]

time: 54.3 us -> 54 us (level)
  no operation moved by 1% of the time
where the time goes in v6:
time: 54 us; the launch traced here: 53.8 us
  starting transfers between devices  15.5 us (29%)
  waiting for transfers between devices  14.5 us (27%)
  other arithmetic  12.8 us (24%)
  Pallas kernels  9.14 us (17%)
  matrix products  0.81 us (2%)
  local copies, waits for them, and re-layouts  0.72 us (1%)
    all_to_all x1, waiting for transfers between devices, body(): blocks = lax.all_to_all(pack(slc_tiles, devices), 'gx', 0, 0, tiled=True)  9.43 us
    ppermute x6, starting transfers between devices, body(): lax.ppermute(sums, 'gx', [(s, s ^ k) for s in range(devices)])  7.95 us
    all_to_all x1, starting transfers between devices, body(): blocks = lax.all_to_all(pack(slc_tiles, devices), 'gx', 0, 0, tiled=True)  7.56 us
    another operation x3, other arithmetic, solve_matrix(): factor = jnp.linalg.cholesky(normal_matrix)  6.52 us
    another operation x2, other arithmetic, solve_matrix(): solved = jax.scipy.linalg.cho_solve((factor, True), columns)  5.55 us
    pallas_call x1, Pallas kernels, observe_all(): pl.pallas_call(functools.partial(observe_kernel, row_count, unit_count),...  5.17 us
    ppermute x6, waiting for transfers between devices, body(): lax.ppermute(sums, 'gx', [(s, s ^ k) for s in range(devices)])  5.11 us
    pallas_call x1, Pallas kernels, pack(): pl.pallas_call(functools.partial(pack_kernel, date_dev, row_count), out_s...  2.84 us
  transfers between devices with their start and end apart: 7, of which 5 were waited for; matrix products, arithmetic and copies ran while one was open for 27% of the time, Pallas kernels for 0%

profile of v6, /device:TPU:0, one launch (start us, length us, event | category | flops | bytes accessed | tf_op | source)
XLA Modules:
  0.0 53.8 jit_solution(7779133897561643409)
XLA Ops:
  0.0 2.8 %pack.1 = bf16[16,272,128]{2,1,0:T(8,128)(2,1)} custom-call(bf16[256,2048]{1,0:T(8,128)(2,1)} %bitcast.26), custom_call_target="tpu_custom_call" | custom-call | tf_op jit(solution)/shard_map/pack/pallas_call | solution.py:264
  2.9 7.6 %all-to-all-start = ((bf16[16,272,128]{2,1,0:T(8,128)(2,1)}), bf16[16,272,128]{2,1,0:T(8,128)(2,1)S(1)}, u32[]{:S(2)}, u32[]{:S(2)}) async-start(bf16[16,272,128]{2,1,0:T(8,128)(2,1)} %pack.1), calls=%async_computation | async-start | bytes 2228224 | tf_op jit(solution)/shard_map/all_to_all | solution.py:347
  10.8 5.8 %cholesky.17 = f32[64,64]{1,0:T(8,128)S(1)} custom-call(f32[64,64]{1,0:T(8,128)S(1)} %fusion.18), custom_call_target="Cholesky" | custom-call | tf_op jit(solution)/shard_map/jit(cholesky)/cholesky | solution.py:324
  16.7 0.6 %compare_reduce_fusion = pred[]{:T(512)} fusion(f32[64]{0:T(128)S(1)} %select_reduce_fusion), kind=kLoop, calls=%fused_computation.59 | loop fusion | flops 127 | bytes 257 | tf_op jit(solution)/shard_map/jit(cholesky)/cholesky | solution.py:324
  17.3 0.7 %fusion.9 = f32[1,64,64]{2,1,0:T(8,128)S(1)} fusion(f32[64,64]{1,0:T(8,128)S(1)} %cholesky.17, pred[]{:T(512)} %compare_reduce_fusion), kind=kLoop, calls=%fused_computation.30 | loop fusion | flops 16384 | bytes 32769 | tf_op jit(solution)/shard_map/jit(_cho_solve)/triangular_solve | solution.py:335
  18.0 0.3 copy.8
  18.3 0.2 fusion.12
  18.6 4.9 %custom-call.10 = f32[1,64,64]{1,2,0:T(8,128)S(1)} custom-call(f32[1,64,64]{2,1,0:T(8,128)S(1)} %fusion.9), custom_call_target="InvertDiagBlocksLowerTriangular" | custom-call | tf_op jit(solution)/shard_map/jit(_cho_solve)/triangular_solve | solution.py:335
  23.9 0.1 subtract_multiply_fusion
  24.0 0.3 fusion.15
  24.3 0.2 subtract_convert_fusion
  24.7 0.3 fusion.3.edge_ref
  25.0 9.4 %all-to-all-done.blocks_ref = bf16[16,272,128]{2,1,0:T(8,128)(2,1)S(1)} async-done(((bf16[16,272,128]{2,1,0:T(8,128)(2,1)}), bf16[16,272,128]{2,1,0:T(8,128)(2,1)S(1)}, u32[]{:S(2)}, u32[]{:S(2)}) %all-to-all-start) | async-done | bytes 1114144 | tf_op jit(solution)/shard_map/all_to_all | solution.py:347
  34.4 5.2 %observe.1 = (f32[2560,128]{1,0:T(8,128)S(1)}, f32[2,64]{1,0:T(2,128)S(1)}) custom-call(bf16[16,272,128]{2,1,0:T(8,128)(2,1)S(1)} %all-to-all-done.blocks_ref, f32[32,128]{1,0:T(8,128)S(1)} %constant_dynamic-slice_fusion.weight_ref, f32[2,128]{1,0:T(2,128)S(1)} %reshape.150.edge_weight_ref, bf16[256,128]{1,0:T(8,128)(2,1)S(1)} %fusion.7.band_ref, ...), custom_call_target="tpu_custom_call" | custom-call | tf_op jit(solution)/shard_map/observe/pallas_call | solution.py:201
  39.6 3.4 %collective-permute-start.2 = (f32[2,64]{1,0:T(2,128)S(1)}, f32[2,64]{1,0:T(2,128)S(1)}, u32[]{:S(2)}, u32[]{:S(2)}) collective-permute-start(f32[2,64]{1,0:T(2,128)S(1)} %get-tuple-element.8), channel_id=1, source_target_pairs={{0,12},{1,13},{2,14},{3,15},{4,8},{5,9},{6,10},{7,11},{8,4},{9,5},... | collective-permute-start | bytes 1544 | tf_op jit(solution)/shard_map/ppermute | solution.py:370
  43.0 2.1 %collective-permute-start.1 = (f32[2,64]{1,0:T(2,128)S(1)}, f32[2,64]{1,0:T(2,128)S(1)}, u32[]{:S(2)}, u32[]{:S(2)}) collective-permute-start(f32[2,64]{1,0:T(2,128)S(1)} %get-tuple-element.8), channel_id=1, source_target_pairs={{0,8},{1,9},{2,10},{3,11},{4,12},{5,13},{6,14},{7,15},{8,0},{9,1},... | collective-permute-start | bytes 1544 | tf_op jit(solution)/shard_map/ppermute | solution.py:370
  45.1 0.5 collective-permute-start
  45.6 1.8 %collective-permute-done.1 = f32[2,64]{1,0:T(2,128)S(1)} collective-permute-done((f32[2,64]{1,0:T(2,128)S(1)}, f32[2,64]{1,0:T(2,128)S(1)}, u32[]{:S(2)}, u32[]{:S(2)}) %collective-permute-start.1) | collective-permute-done | bytes 544 | tf_op jit(solution)/shard_map/ppermute | solution.py:370
  47.5 1.2 %collective-permute-done = f32[2,64]{1,0:T(2,128)S(1)} collective-permute-done((f32[2,64]{1,0:T(2,128)S(1)}, f32[2,64]{1,0:T(2,128)S(1)}, u32[]{:S(2)}, u32[]{:S(2)}) %collective-permute-start) | collective-permute-done | bytes 544 | tf_op jit(solution)/shard_map/ppermute | solution.py:370
  48.7 0.3 collective-permute-start.5
  49.1 1.5 %collective-permute-start.4 = (f32[2,64]{1,0:T(2,128)S(1)}, f32[2,64]{1,0:T(2,128)S(1)}, u32[]{:S(2)}, u32[]{:S(2)}) collective-permute-start(f32[2,64]{1,0:T(2,128)S(1)} %add_add_fusion.sums_ref), channel_id=1, source_target_pairs={{0,2},{1,3},{2,0},{3,1},{4,6},{5,7},{6,4},{7,5},{8,10},{9,11},{10,... | collective-permute-start | bytes 1544 | tf_op jit(solution)/shard_map/ppermute | solution.py:370
  50.6 1.1 %collective-permute-done.5 = f32[2,64]{1,0:T(2,128)S(1)} collective-permute-done((f32[2,64]{1,0:T(2,128)S(1)}, f32[2,64]{1,0:T(2,128)S(1)}, u32[]{:S(2)}, u32[]{:S(2)}) %collective-permute-start.5) | collective-permute-done | bytes 544 | tf_op jit(solution)/shard_map/ppermute | solution.py:370
  51.7 0.9 %collective-permute-done.4 = f32[2,64]{1,0:T(2,128)S(1)} collective-permute-done((f32[2,64]{1,0:T(2,128)S(1)}, f32[2,64]{1,0:T(2,128)S(1)}, u32[]{:S(2)}, u32[]{:S(2)}) %collective-permute-start.4) | collective-permute-done | bytes 544 | tf_op jit(solution)/shard_map/ppermute | solution.py:370
  52.6 1.1 %remove.1 = f32[2048,128]{1,0:T(8,128)} custom-call(f32[2560,128]{1,0:T(8,128)S(1)} %get-tuple-element.7.series_ref, f32[2,64]{1,0:T(2,128)S(1)} %add_add_fusion.sums_ref, f32[3,2,64]{2,1,0:T(2,128)S(1)} %pad_maximum_fusion.2.more_ref, f32[1,128]{1,0:T(1,128)S(1)} %multiply_add_fusion.1.coord_ref), custom_call_target="tpu_custom_call" | custom-call | tf_op jit(solution)/shard_map/remove/pallas_call | solution.py:306
  (33 shorter events, 0.9 us)
Async XLA Ops:
  2.9 7.6 %copy-start.1 = (s32[192,2]{0,1:T(2,128)S(1)}, s32[192,2]{0,1:T(2,128)}, u32[]{:S(2)}) copy-start(s32[192,2]{0,1:T(2,128)} %param.5) | copy-start | bytes 4612
  2.9 15.1 %copy-start = (f32[32,2048]{1,0:T(8,128)S(1)}, f32[32,2048]{1,0:T(8,128)}, u32[]{:S(2)}) copy-start(f32[32,2048]{1,0:T(8,128)} %param.4) | copy-start | bytes 786436
  2.9 31.5 %all-to-all-start = ((bf16[16,272,128]{2,1,0:T(8,128)(2,1)}), bf16[16,272,128]{2,1,0:T(8,128)(2,1)S(1)}, u32[]{:S(2)}, u32[]{:S(2)}) async-start(bf16[16,272,128]{2,1,0:T(8,128)(2,1)} %pack.1), calls=%async_computation | async-start | bytes 2228224 | tf_op jit(solution)/shard_map/all_to_all | solution.py:347
  39.6 6.1 %collective-permute-start.2 = (f32[2,64]{1,0:T(2,128)S(1)}, f32[2,64]{1,0:T(2,128)S(1)}, u32[]{:S(2)}, u32[]{:S(2)}) collective-permute-start(f32[2,64]{1,0:T(2,128)S(1)} %get-tuple-element.8), channel_id=1, source_target_pairs={{0,12},{1,13},{2,14},{3,15},{4,8},{5,9},{6,10},{7,11},{8,4},{9,5},... | collective-permute-start | bytes 1544 | tf_op jit(solution)/shard_map/ppermute | solution.py:370
  43.0 4.5 %collective-permute-start.1 = (f32[2,64]{1,0:T(2,128)S(1)}, f32[2,64]{1,0:T(2,128)S(1)}, u32[]{:S(2)}, u32[]{:S(2)}) collective-permute-start(f32[2,64]{1,0:T(2,128)S(1)} %get-tuple-element.8), channel_id=1, source_target_pairs={{0,8},{1,9},{2,10},{3,11},{4,12},{5,13},{6,14},{7,15},{8,0},{9,1},... | collective-permute-start | bytes 1544 | tf_op jit(solution)/shard_map/ppermute | solution.py:370
  45.1 3.6 %collective-permute-start = (f32[2,64]{1,0:T(2,128)S(1)}, f32[2,64]{1,0:T(2,128)S(1)}, u32[]{:S(2)}, u32[]{:S(2)}) collective-permute-start(f32[2,64]{1,0:T(2,128)S(1)} %get-tuple-element.8), channel_id=1, source_target_pairs={{0,4},{1,5},{2,6},{3,7},{4,0},{5,1},{6,2},{7,3},{8,12},{9,13},{10,... | collective-permute-start | bytes 1544 | tf_op jit(solution)/shard_map/ppermute | solution.py:370
  48.7 3.0 %collective-permute-start.5 = (f32[2,64]{1,0:T(2,128)S(1)}, f32[2,64]{1,0:T(2,128)S(1)}, u32[]{:S(2)}, u32[]{:S(2)}) collective-permute-start(f32[2,64]{1,0:T(2,128)S(1)} %add_add_fusion.sums_ref), channel_id=1, source_target_pairs={{0,3},{1,2},{2,1},{3,0},{4,7},{5,6},{6,5},{7,4},{8,11},{9,10},{10,... | collective-permute-start | bytes 1544 | tf_op jit(solution)/shard_map/ppermute | solution.py:370
  49.1 3.6 %collective-permute-start.4 = (f32[2,64]{1,0:T(2,128)S(1)}, f32[2,64]{1,0:T(2,128)S(1)}, u32[]{:S(2)}, u32[]{:S(2)}) collective-permute-start(f32[2,64]{1,0:T(2,128)S(1)} %add_add_fusion.sums_ref), channel_id=1, source_target_pairs={{0,2},{1,3},{2,0},{3,1},{4,6},{5,7},{6,4},{7,5},{8,10},{9,11},{10,... | collective-permute-start | bytes 1544 | tf_op jit(solution)/shard_map/ppermute | solution.py:370
  50.6 2.1 %collective-permute-start.3 = (f32[2,64]{1,0:T(2,128)S(1)}, f32[2,64]{1,0:T(2,128)S(1)}, u32[]{:S(2)}, u32[]{:S(2)}) collective-permute-start(f32[2,64]{1,0:T(2,128)S(1)} %add_add_fusion.sums_ref), channel_id=1, source_target_pairs={{0,1},{1,0},{2,3},{3,2},{4,5},{5,4},{6,7},{7,6},{8,9},{9,8},{10,11... | collective-permute-start | bytes 1544 | tf_op jit(solution)/shard_map/ppermute | solution.py:370

commit v7 on v6

--- a/solution.py
+++ b/solution.py
@@ -134,7 +134,7 @@
 
     combos = unit_count * SUB * LAGS
 
-    together = 3 if (unit_count + 1) % 3 == 0 else 2
+    together = 9 if (unit_count + 1) % 9 == 0 else 3
 
     def bring_some(step, carry):
         for g in range(together):
@@ -302,7 +302,7 @@
 
 
 def remove_trend(series, sums, more, coord, rows, pixels, square_sum):
-    chunks = 8
+    chunks = 4
     return pl.pallas_call(
         functools.partial(remove_kernel, pixels, square_sum),
         out_shape=jax.ShapeDtypeStruct((rows, LANES), F32),

time: 54 us -> 53.8 us (level)
  no operation moved by 1% of the time
where the time goes in v7:
time: 53.8 us; the launch traced here: 53.5 us
  starting transfers between devices  15.5 us (29%)
  waiting for transfers between devices  14.5 us (27%)
  other arithmetic  12.8 us (24%)
  Pallas kernels  8.9 us (17%)
  matrix products  0.81 us (2%)
  local copies, waits for them, and re-layouts  0.72 us (1%)
    all_to_all x1, waiting for transfers between devices, body(): blocks = lax.all_to_all(pack(slc_tiles, devices), 'gx', 0, 0, tiled=True)  9.43 us
    ppermute x6, starting transfers between devices, body(): lax.ppermute(sums, 'gx', [(s, s ^ k) for s in range(devices)])  7.95 us
    all_to_all x1, starting transfers between devices, body(): blocks = lax.all_to_all(pack(slc_tiles, devices), 'gx', 0, 0, tiled=True)  7.56 us
    another operation x3, other arithmetic, solve_matrix(): factor = jnp.linalg.cholesky(normal_matrix)  6.52 us
    another operation x2, other arithmetic, solve_matrix(): solved = jax.scipy.linalg.cho_solve((factor, True), columns)  5.55 us
    ppermute x6, waiting for transfers between devices, body(): lax.ppermute(sums, 'gx', [(s, s ^ k) for s in range(devices)])  5.11 us
    pallas_call x1, Pallas kernels, observe_all(): pl.pallas_call(functools.partial(observe_kernel, row_count, unit_count),...  4.96 us
    pallas_call x1, Pallas kernels, pack(): pl.pallas_call(functools.partial(pack_kernel, date_dev, row_count), out_s...  2.84 us
  transfers between devices with their start and end apart: 7, of which 5 were waited for; matrix products, arithmetic and copies ran while one was open for 27% of the time, Pallas kernels for 0%

profile of v7, /device:TPU:0, one launch (start us, length us, event | category | flops | bytes accessed | tf_op | source)
XLA Modules:
  0.0 53.5 jit_solution(8901977951035080042)
XLA Ops:
  0.0 2.8 %pack.1 = bf16[16,272,128]{2,1,0:T(8,128)(2,1)} custom-call(bf16[256,2048]{1,0:T(8,128)(2,1)} %bitcast.26), custom_call_target="tpu_custom_call" | custom-call | tf_op jit(solution)/shard_map/pack/pallas_call | solution.py:264
  2.9 7.6 %all-to-all-start = ((bf16[16,272,128]{2,1,0:T(8,128)(2,1)}), bf16[16,272,128]{2,1,0:T(8,128)(2,1)S(1)}, u32[]{:S(2)}, u32[]{:S(2)}) async-start(bf16[16,272,128]{2,1,0:T(8,128)(2,1)} %pack.1), calls=%async_computation | async-start | bytes 2228224 | tf_op jit(solution)/shard_map/all_to_all | solution.py:347
  10.8 5.8 %cholesky.17 = f32[64,64]{1,0:T(8,128)S(1)} custom-call(f32[64,64]{1,0:T(8,128)S(1)} %fusion.18), custom_call_target="Cholesky" | custom-call | tf_op jit(solution)/shard_map/jit(cholesky)/cholesky | solution.py:324
  16.7 0.6 %compare_reduce_fusion = pred[]{:T(512)} fusion(f32[64]{0:T(128)S(1)} %select_reduce_fusion), kind=kLoop, calls=%fused_computation.59 | loop fusion | flops 127 | bytes 257 | tf_op jit(solution)/shard_map/jit(cholesky)/cholesky | solution.py:324
  17.3 0.7 %fusion.9 = f32[1,64,64]{2,1,0:T(8,128)S(1)} fusion(f32[64,64]{1,0:T(8,128)S(1)} %cholesky.17, pred[]{:T(512)} %compare_reduce_fusion), kind=kLoop, calls=%fused_computation.30 | loop fusion | flops 16384 | bytes 32769 | tf_op jit(solution)/shard_map/jit(_cho_solve)/triangular_solve | solution.py:335
  18.0 0.3 copy.8
  18.3 0.2 fusion.12
  18.6 4.9 %custom-call.10 = f32[1,64,64]{1,2,0:T(8,128)S(1)} custom-call(f32[1,64,64]{2,1,0:T(8,128)S(1)} %fusion.9), custom_call_target="InvertDiagBlocksLowerTriangular" | custom-call | tf_op jit(solution)/shard_map/jit(_cho_solve)/triangular_solve | solution.py:335
  23.9 0.1 subtract_multiply_fusion
  24.0 0.3 fusion.15
  24.3 0.2 subtract_convert_fusion
  24.7 0.3 fusion.3.edge_ref
  25.0 9.4 %all-to-all-done.blocks_ref = bf16[16,272,128]{2,1,0:T(8,128)(2,1)S(1)} async-done(((bf16[16,272,128]{2,1,0:T(8,128)(2,1)}), bf16[16,272,128]{2,1,0:T(8,128)(2,1)S(1)}, u32[]{:S(2)}, u32[]{:S(2)}) %all-to-all-start) | async-done | bytes 1114144 | tf_op jit(solution)/shard_map/all_to_all | solution.py:347
  34.4 5.0 %observe.1 = (f32[2560,128]{1,0:T(8,128)S(1)}, f32[2,64]{1,0:T(2,128)S(1)}) custom-call(bf16[16,272,128]{2,1,0:T(8,128)(2,1)S(1)} %all-to-all-done.blocks_ref, f32[32,128]{1,0:T(8,128)S(1)} %constant_dynamic-slice_fusion.weight_ref, f32[2,128]{1,0:T(2,128)S(1)} %reshape.150.edge_weight_ref, bf16[256,128]{1,0:T(8,128)(2,1)S(1)} %fusion.7.band_ref, ...), custom_call_target="tpu_custom_call" | custom-call | tf_op jit(solution)/shard_map/observe/pallas_call | solution.py:201
  39.4 3.4 %collective-permute-start.2 = (f32[2,64]{1,0:T(2,128)S(1)}, f32[2,64]{1,0:T(2,128)S(1)}, u32[]{:S(2)}, u32[]{:S(2)}) collective-permute-start(f32[2,64]{1,0:T(2,128)S(1)} %get-tuple-element.8), channel_id=1, source_target_pairs={{0,12},{1,13},{2,14},{3,15},{4,8},{5,9},{6,10},{7,11},{8,4},{9,5},... | collective-permute-start | bytes 1544 | tf_op jit(solution)/shard_map/ppermute | solution.py:370
  42.8 2.1 %collective-permute-start.1 = (f32[2,64]{1,0:T(2,128)S(1)}, f32[2,64]{1,0:T(2,128)S(1)}, u32[]{:S(2)}, u32[]{:S(2)}) collective-permute-start(f32[2,64]{1,0:T(2,128)S(1)} %get-tuple-element.8), channel_id=1, source_target_pairs={{0,8},{1,9},{2,10},{3,11},{4,12},{5,13},{6,14},{7,15},{8,0},{9,1},... | collective-permute-start | bytes 1544 | tf_op jit(solution)/shard_map/ppermute | solution.py:370
  44.9 0.5 collective-permute-start
  45.4 1.8 %collective-permute-done.1 = f32[2,64]{1,0:T(2,128)S(1)} collective-permute-done((f32[2,64]{1,0:T(2,128)S(1)}, f32[2,64]{1,0:T(2,128)S(1)}, u32[]{:S(2)}, u32[]{:S(2)}) %collective-permute-start.1) | collective-permute-done | bytes 544 | tf_op jit(solution)/shard_map/ppermute | solution.py:370
  47.2 1.2 %collective-permute-done = f32[2,64]{1,0:T(2,128)S(1)} collective-permute-done((f32[2,64]{1,0:T(2,128)S(1)}, f32[2,64]{1,0:T(2,128)S(1)}, u32[]{:S(2)}, u32[]{:S(2)}) %collective-permute-start) | collective-permute-done | bytes 544 | tf_op jit(solution)/shard_map/ppermute | solution.py:370
  48.5 0.3 collective-permute-start.5
  48.8 1.5 %collective-permute-start.4 = (f32[2,64]{1,0:T(2,128)S(1)}, f32[2,64]{1,0:T(2,128)S(1)}, u32[]{:S(2)}, u32[]{:S(2)}) collective-permute-start(f32[2,64]{1,0:T(2,128)S(1)} %add_add_fusion.sums_ref), channel_id=1, source_target_pairs={{0,2},{1,3},{2,0},{3,1},{4,6},{5,7},{6,4},{7,5},{8,10},{9,11},{10,... | collective-permute-start | bytes 1544 | tf_op jit(solution)/shard_map/ppermute | solution.py:370
  50.4 1.1 %collective-permute-done.5 = f32[2,64]{1,0:T(2,128)S(1)} collective-permute-done((f32[2,64]{1,0:T(2,128)S(1)}, f32[2,64]{1,0:T(2,128)S(1)}, u32[]{:S(2)}, u32[]{:S(2)}) %collective-permute-start.5) | collective-permute-done | bytes 544 | tf_op jit(solution)/shard_map/ppermute | solution.py:370
  51.5 0.9 %collective-permute-done.4 = f32[2,64]{1,0:T(2,128)S(1)} collective-permute-done((f32[2,64]{1,0:T(2,128)S(1)}, f32[2,64]{1,0:T(2,128)S(1)}, u32[]{:S(2)}, u32[]{:S(2)}) %collective-permute-start.4) | collective-permute-done | bytes 544 | tf_op jit(solution)/shard_map/ppermute | solution.py:370
  52.4 1.1 %remove.1 = f32[2048,128]{1,0:T(8,128)} custom-call(f32[2560,128]{1,0:T(8,128)S(1)} %get-tuple-element.7.series_ref, f32[2,64]{1,0:T(2,128)S(1)} %add_add_fusion.sums_ref, f32[3,2,64]{2,1,0:T(2,128)S(1)} %pad_maximum_fusion.2.more_ref, f32[1,128]{1,0:T(1,128)S(1)} %multiply_add_fusion.1.coord_ref), custom_call_target="tpu_custom_call" | custom-call | tf_op jit(solution)/shard_map/remove/pallas_call | solution.py:306
  (33 shorter events, 0.9 us)
Async XLA Ops:
  2.9 7.6 %copy-start.1 = (s32[192,2]{0,1:T(2,128)S(1)}, s32[192,2]{0,1:T(2,128)}, u32[]{:S(2)}) copy-start(s32[192,2]{0,1:T(2,128)} %param.5) | copy-start | bytes 4612
  2.9 15.1 %copy-start = (f32[32,2048]{1,0:T(8,128)S(1)}, f32[32,2048]{1,0:T(8,128)}, u32[]{:S(2)}) copy-start(f32[32,2048]{1,0:T(8,128)} %param.4) | copy-start | bytes 786436
  2.9 31.5 %all-to-all-start = ((bf16[16,272,128]{2,1,0:T(8,128)(2,1)}), bf16[16,272,128]{2,1,0:T(8,128)(2,1)S(1)}, u32[]{:S(2)}, u32[]{:S(2)}) async-start(bf16[16,272,128]{2,1,0:T(8,128)(2,1)} %pack.1), calls=%async_computation | async-start | bytes 2228224 | tf_op jit(solution)/shard_map/all_to_all | solution.py:347
  39.4 6.1 %collective-permute-start.2 = (f32[2,64]{1,0:T(2,128)S(1)}, f32[2,64]{1,0:T(2,128)S(1)}, u32[]{:S(2)}, u32[]{:S(2)}) collective-permute-start(f32[2,64]{1,0:T(2,128)S(1)} %get-tuple-element.8), channel_id=1, source_target_pairs={{0,12},{1,13},{2,14},{3,15},{4,8},{5,9},{6,10},{7,11},{8,4},{9,5},... | collective-permute-start | bytes 1544 | tf_op jit(solution)/shard_map/ppermute | solution.py:370
  42.8 4.5 %collective-permute-start.1 = (f32[2,64]{1,0:T(2,128)S(1)}, f32[2,64]{1,0:T(2,128)S(1)}, u32[]{:S(2)}, u32[]{:S(2)}) collective-permute-start(f32[2,64]{1,0:T(2,128)S(1)} %get-tuple-element.8), channel_id=1, source_target_pairs={{0,8},{1,9},{2,10},{3,11},{4,12},{5,13},{6,14},{7,15},{8,0},{9,1},... | collective-permute-start | bytes 1544 | tf_op jit(solution)/shard_map/ppermute | solution.py:370
  44.9 3.6 %collective-permute-start = (f32[2,64]{1,0:T(2,128)S(1)}, f32[2,64]{1,0:T(2,128)S(1)}, u32[]{:S(2)}, u32[]{:S(2)}) collective-permute-start(f32[2,64]{1,0:T(2,128)S(1)} %get-tuple-element.8), channel_id=1, source_target_pairs={{0,4},{1,5},{2,6},{3,7},{4,0},{5,1},{6,2},{7,3},{8,12},{9,13},{10,... | collective-permute-start | bytes 1544 | tf_op jit(solution)/shard_map/ppermute | solution.py:370
  48.5 3.0 %collective-permute-start.5 = (f32[2,64]{1,0:T(2,128)S(1)}, f32[2,64]{1,0:T(2,128)S(1)}, u32[]{:S(2)}, u32[]{:S(2)}) collective-permute-start(f32[2,64]{1,0:T(2,128)S(1)} %add_add_fusion.sums_ref), channel_id=1, source_target_pairs={{0,3},{1,2},{2,1},{3,0},{4,7},{5,6},{6,5},{7,4},{8,11},{9,10},{10,... | collective-permute-start | bytes 1544 | tf_op jit(solution)/shard_map/ppermute | solution.py:370
  48.8 3.6 %collective-permute-start.4 = (f32[2,64]{1,0:T(2,128)S(1)}, f32[2,64]{1,0:T(2,128)S(1)}, u32[]{:S(2)}, u32[]{:S(2)}) collective-permute-start(f32[2,64]{1,0:T(2,128)S(1)} %add_add_fusion.sums_ref), channel_id=1, source_target_pairs={{0,2},{1,3},{2,0},{3,1},{4,6},{5,7},{6,4},{7,5},{8,10},{9,11},{10,... | collective-permute-start | bytes 1544 | tf_op jit(solution)/shard_map/ppermute | solution.py:370
  50.4 2.1 %collective-permute-start.3 = (f32[2,64]{1,0:T(2,128)S(1)}, f32[2,64]{1,0:T(2,128)S(1)}, u32[]{:S(2)}, u32[]{:S(2)}) collective-permute-start(f32[2,64]{1,0:T(2,128)S(1)} %add_add_fusion.sums_ref), channel_id=1, source_target_pairs={{0,1},{1,0},{2,3},{3,2},{4,5},{5,4},{6,7},{7,6},{8,9},{9,8},{10,11... | collective-permute-start | bytes 1544 | tf_op jit(solution)/shard_map/ppermute | solution.py:370
